TPU v7x, 32 devices: a whole 2x2x4 slice. The times are simulated.
32 devices in a mesh: pipe: 4 (over x, core), seq: 8 (over z, y).
Axes of the slice: x: 2, y: 2, z: 4, core: 2. Of those that a mesh axis runs over, the one named last changes fastest.
Arguments:
- value_in: bfloat16 [4, 1024, 4096], P('pipe', 'seq'), may hold values from -6 to 6
- gate_one: bfloat16 [4, 1024, 4096], P('pipe', 'seq'), may hold values from -6 to 6
- gate_two: bfloat16 [4, 1024, 4096], P('pipe', 'seq'), may hold values from -6 to 6
- out_grad: bfloat16 [4, 1024, 4096], P('pipe', 'seq'), may hold values from -6 to 6
- w_embed: float32 [4, 33, 64], P('pipe'), may hold values from -1 to 1
- b_embed: float32 [4, 64], P('pipe'), may hold values from -4 to 4
- w_filter: float32 [4, 64, 4096], P('pipe', None, 'seq'), may hold values from -0.75 to 0.75
- decay: float32 [4, 4096], P('pipe', 'seq'), may hold values from 0.3 to 128
- skip: float32 [4, 4096], P('pipe', 'seq'), may hold values from -4 to 4
Outputs:
- next_input: bfloat16 [4, 1024, 4096], P('pipe', 'seq')
- grad_value: bfloat16 [4, 1024, 4096], P('pipe', 'seq')
- grad_gate_one: bfloat16 [4, 1024, 4096], P('pipe', 'seq')
- grad_gate_two: bfloat16 [4, 1024, 4096], P('pipe', 'seq')
- grad_w_embed: float32 [4, 33, 64], P('pipe')
- grad_b_embed: float32 [4, 64], P('pipe')
- grad_w_filter: float32 [4, 64, 4096], P('pipe', None, 'seq')
- grad_decay: float32 [4, 4096], P('pipe', 'seq')
- grad_skip: float32 [4, 4096], P('pipe', 'seq')
All inputs are finite; a program needn't handle non-finite values.
Results may differ from a plain program's by a relative error of at most 0.0058.
Values may be sent and summed in bfloat16 or wider, within the bound.
A program may use at most 128 MiB of HBM per device.

v0:
```python
import math

import jax
import jax.numpy as jnp
from jax import lax
from jax.sharding import PartitionSpec as P

E = 33


def from_behind(value, axis, steps):
    count = lax.axis_size(axis)
    pairs = [(source, (source + steps) % count) for source in range(count)]
    return lax.ppermute(value, axis, pairs)


def contract(form, left, right):
    return jnp.einsum(form, left, right, precision=lax.Precision.HIGHEST)


def position_features(length):
    position_ids = jnp.arange(length, dtype=jnp.int32)
    band_count = (E - 1) // 2
    band_index = jnp.arange(1, band_count + 1, dtype=jnp.int32)
    turn_ids = band_index[:, None] * band_index[:, None] * position_ids[None, :] % length
    angles = 2.0 * math.pi / length * turn_ids.astype(jnp.float32)
    position_ramp = position_ids.astype(jnp.float32)[None, :] / length
    return jnp.concatenate([position_ramp, jnp.cos(angles), jnp.sin(angles)], axis=0)


def build_tables(length):
    fft_total = 2 * length
    outer_len = 128
    half_len = outer_len // 2
    kept_len = half_len + 1
    inner_len = fft_total // outer_len
    index_kept = jnp.arange(kept_len, dtype=jnp.int32)
    index_half = jnp.arange(half_len, dtype=jnp.int32)
    index_inner = jnp.arange(inner_len, dtype=jnp.int32)
    angle_outer = (
        2.0
        * math.pi
        / outer_len
        * (index_kept[:, None] * index_half[None, :] % outer_len).astype(jnp.float32)
    )
    cos_outer = jnp.cos(angle_outer)
    sin_outer = jnp.sin(angle_outer)
    table_first = jnp.concatenate([cos_outer, -sin_outer], axis=0)
    angle_twist = (
        2.0
        * math.pi
        / fft_total
        * (index_kept[:, None] * index_inner[None, :] % fft_total).astype(jnp.float32)
    )
    cos_twist = jnp.cos(angle_twist)[:, :, None]
    sin_twist = jnp.sin(angle_twist)[:, :, None]
    angle_inner = (
        2.0
        * math.pi
        / inner_len
        * (index_inner[:, None] * index_inner[None, :] % inner_len).astype(jnp.float32)
    )
    cos_inner = jnp.cos(angle_inner)
    sin_inner = jnp.sin(angle_inner)
    table_second = jnp.stack(
        [jnp.stack([cos_inner, sin_inner], axis=1), jnp.stack([-sin_inner, cos_inner], axis=1)],
        axis=0,
    )
    table_back = jnp.stack(
        [jnp.stack([cos_inner, -sin_inner], axis=1), jnp.stack([sin_inner, cos_inner], axis=1)],
        axis=0,
    )
    weight_kept = (
        jnp.where((index_kept == 0) | (index_kept == half_len), 1.0, 2.0).astype(jnp.float32)
        / fft_total
    )
    table_last = jnp.stack(
        [
            jnp.transpose(cos_outer) * weight_kept[None, :],
            -jnp.transpose(sin_outer) * weight_kept[None, :],
        ],
        axis=1,
    )
    return (
        table_first,
        cos_twist,
        sin_twist,
        table_second,
        table_back,
        table_last,
        half_len,
        kept_len,
        inner_len,
    )


def forward_transform(field, tables_all):
    (
        table_first,
        cos_twist,
        sin_twist,
        table_second,
        table_back,
        table_last,
        half_len,
        kept_len,
        inner_len,
    ) = tables_all
    columns = field.shape[1]
    shaped = field.reshape(half_len, inner_len, columns)
    stacked = contract("kn,npc->kpc", table_first, shaped)
    part_re = stacked[:kept_len]
    part_im = stacked[kept_len:]
    twisted = jnp.stack(
        [part_re * cos_twist + part_im * sin_twist, part_im * cos_twist - part_re * sin_twist],
        axis=0,
    )
    return contract("sqrp,rkpc->skqc", table_second, twisted)


def inverse_transform(spec, tables_all):
    (
        table_first,
        cos_twist,
        sin_twist,
        table_second,
        table_back,
        table_last,
        half_len,
        kept_len,
        inner_len,
    ) = tables_all
    columns = spec.shape[3]
    sectioned = contract("sprq,rkqc->skpc", table_back, spec)
    section_re = sectioned[0]
    section_im = sectioned[1]
    twisted = jnp.stack(
        [
            section_re * cos_twist - section_im * sin_twist,
            section_im * cos_twist + section_re * sin_twist,
        ],
        axis=0,
    )
    result = contract("nrk,rkpc->npc", table_last, twisted)
    return result.reshape(half_len * inner_len, columns)


def spectral_product(left, right, conjugate_left):
    left_re = left[0]
    left_im = left[1]
    right_re = right[0]
    right_im = right[1]
    if conjugate_left:
        left_im = -left_im
    return jnp.stack(
        [left_re * right_re - left_im * right_im, left_re * right_im + left_im * right_re], axis=0
    )


def per_device(value_in, gate_one, gate_two, out_grad, w_embed, b_embed, w_filter, decay, skip):
    values = value_in[0]
    gate_first = gate_one[0]
    gate_second = gate_two[0]
    cotangent = out_grad[0]
    filter_w = w_filter[0]
    shards = lax.axis_size("seq")
    length = values.shape[0] * shards
    weighted = (values.astype(jnp.float32) * gate_first.astype(jnp.float32)).astype(jnp.bfloat16)
    upstream = (cotangent.astype(jnp.float32) * gate_second.astype(jnp.float32)).astype(
        jnp.bfloat16
    )
    features = position_features(length)
    preact = contract("ef,et->ft", w_embed[0], features) + b_embed[0][:, None]
    activation = jnp.sin(preact)
    positions = jnp.arange(length, dtype=jnp.int32).astype(jnp.float32)[:, None]
    envelope = jnp.exp(-decay[0][None, :] * positions / length) * (1.0 / math.sqrt(length))
    kernel = contract("ft,fc->tc", activation, filter_w) * envelope
    tables_all = build_tables(length)
    kernel_spec = forward_transform(kernel, tables_all)
    skip_row = skip[0][None, :]
    weighted_chan, upstream_chan = (
        lax.all_to_all(weighted, "seq", split_axis=1, concat_axis=0, tiled=True),
        lax.all_to_all(upstream, "seq", split_axis=1, concat_axis=0, tiled=True),
    )
    weighted_f = weighted_chan.astype(jnp.float32)
    weighted_spec = forward_transform(weighted_f, tables_all)
    conv = inverse_transform(spectral_product(kernel_spec, weighted_spec, False), tables_all)
    mixed_chan, weighted_f, weighted_spec = (
        (conv + skip_row * weighted_f).astype(jnp.bfloat16),
        weighted_f,
        weighted_spec,
    )
    upstream_f = upstream_chan.astype(jnp.float32)
    upstream_spec = forward_transform(upstream_f, tables_all)
    backward_conv = inverse_transform(
        spectral_product(kernel_spec, upstream_spec, True), tables_all
    )
    grad_chan = (backward_conv + skip_row * upstream_f).astype(jnp.bfloat16)
    grad_skip = jnp.sum(upstream_f * weighted_f, axis=0)
    grad_kernel = inverse_transform(
        spectral_product(weighted_spec, upstream_spec, True), tables_all
    )
    grad_chan, grad_skip, grad_kernel = (grad_chan, grad_skip, grad_kernel)
    mixed_seq, grad_weighted = (
        lax.all_to_all(mixed_chan, "seq", split_axis=0, concat_axis=1, tiled=True),
        lax.all_to_all(grad_chan, "seq", split_axis=0, concat_axis=1, tiled=True),
    )
    output = (gate_second.astype(jnp.float32) * mixed_seq.astype(jnp.float32)).astype(jnp.bfloat16)
    next_input = from_behind(output, "pipe", 1)
    grad_decay = jnp.sum(grad_kernel * kernel * (-positions / length), axis=0)
    grad_raw = grad_kernel * envelope
    grad_filter_w = contract("ft,tc->fc", activation, grad_raw)
    grad_preact = contract("fc,tc->ft", filter_w, grad_raw) * jnp.cos(preact)
    part_weight = contract("et,ft->ef", features, grad_preact)
    part_bias = jnp.sum(grad_preact, axis=1)
    grad_embed_w, grad_embed_b = lax.psum((part_weight, part_bias), "seq")
    grad_values = (grad_weighted.astype(jnp.float32) * gate_first.astype(jnp.float32)).astype(
        jnp.bfloat16
    )
    grad_first = (grad_weighted.astype(jnp.float32) * values.astype(jnp.float32)).astype(
        jnp.bfloat16
    )
    grad_second = (cotangent.astype(jnp.float32) * mixed_seq.astype(jnp.float32)).astype(
        jnp.bfloat16
    )
    moved_values, moved_first, moved_second = from_behind(
        (grad_values, grad_first, grad_second), "pipe", -1
    )
    return (
        next_input[None],
        moved_values[None],
        moved_first[None],
        moved_second[None],
        grad_embed_w[None],
        grad_embed_b[None],
        grad_filter_w[None],
        grad_decay[None],
        grad_skip[None],
    )


def solution(mesh):
    return jax.shard_map(
        per_device,
        mesh=mesh,
        in_specs=(
            P("pipe", "seq", None),
            P("pipe", "seq", None),
            P("pipe", "seq", None),
            P("pipe", "seq", None),
            P("pipe", None, None),
            P("pipe", None),
            P("pipe", None, "seq"),
            P("pipe", "seq"),
            P("pipe", "seq"),
        ),
        out_specs=(
            P("pipe", "seq", None),
            P("pipe", "seq", None),
            P("pipe", "seq", None),
            P("pipe", "seq", None),
            P("pipe", None, None),
            P("pipe", None),
            P("pipe", None, "seq"),
            P("pipe", "seq"),
            P("pipe", "seq"),
        ),
        check_vma=False,
    )
```

profile of v0, /device:TPU:0, one launch (start us, length us, event | category | flops | bytes accessed | tf_op | source)
XLA Modules:
  0.0 283.4 jit_solution(16916964960619495326)
XLA Ops:
  4.4 7.3 %all-to-all-start.2 = ((bf16[128,8,512]{0,2,1:T(8,128)(2,1)}), bf16[128,8,512]{0,2,1:T(8,128)(2,1)}, u32[]{:S(2)}, u32[]{:S(2)}) async-start(bf16[128,8,512]{0,2,1:T(8,128)(2,1)} %bitcast.43), calls=%async_computation.2 | async-start | bytes 2097152 | tf_op jit(solution)/shard_map/all_to_all | solution.py:183
  20.5 17.0 %all-to-all-done.2 = bf16[128,8,512]{0,2,1:T(8,128)(2,1)} async-done(((bf16[128,8,512]{0,2,1:T(8,128)(2,1)}), bf16[128,8,512]{0,2,1:T(8,128)(2,1)}, u32[]{:S(2)}, u32[]{:S(2)}) %all-to-all-start.2) | async-done | bytes 1048608 | tf_op jit(solution)/shard_map/all_to_all | solution.py:183
  37.5 3.8 %all-to-all-start = ((bf16[128,8,512]{0,2,1:T(8,128)(2,1)}), bf16[128,8,512]{0,2,1:T(8,128)(2,1)S(1)}, u32[]{:S(2)}, u32[]{:S(2)}) async-start(bf16[128,8,512]{0,2,1:T(8,128)(2,1)} %bitcast.199), calls=%async_computation | async-start | bytes 2097152 | tf_op jit(solution)/shard_map/all_to_all | solution.py:182
  45.8 2.8 fusion.52
  48.7 6.2 %fusion.50 = f32[130,16,512]{2,0,1:T(8,128)} fusion(f32[64,16,512]{2,1,0:T(8,128)S(1)} %bitcast.195, f32[65,64]{0,1:T(8,128)S(1)} %get-tuple-element.91, f32[65,64]{0,1:T(8,128)S(1)} %get-tuple-element.92), kind=kOutput, calls=%fused_computation.82 | convolution fusion | flops 817897600 | bytes 6390272 | tf_op jit(solution)/shard_map/kn,npc->kpc/dot_general | solution.py:18
  56.4 4.9 %fusion.62 = f32[130,16,512]{2,0,1:T(8,128)} fusion(bf16[64,16,512]{2,1,0:T(8,128)(2,1)S(1)} %bitcast.201, f32[65,64]{0,1:T(8,128)S(1)} %get-tuple-element.91, f32[65,64]{0,1:T(8,128)S(1)} %get-tuple-element.92), kind=kOutput, calls=%fused_computation.94 | convolution fusion | flops 817897600 | bytes 5341696 | tf_op jit(solution)/shard_map/kn,npc->kpc/dot_general | solution.py:18
  61.2 6.0 %all-to-all-done = bf16[128,8,512]{0,2,1:T(8,128)(2,1)S(1)} async-done(((bf16[128,8,512]{0,2,1:T(8,128)(2,1)}), bf16[128,8,512]{0,2,1:T(8,128)(2,1)S(1)}, u32[]{:S(2)}, u32[]{:S(2)}) %all-to-all-start) | async-done | bytes 1048608 | tf_op jit(solution)/shard_map/all_to_all | solution.py:182
  67.8 2.7 fusion.64
  70.6 5.0 %add_bitcast_fusion = (f32[1,65,16,512]{3,1,2,0:T(8,128)S(1)}, f32[1,65,16,512]{3,1,2,0:T(8,128)S(1)}, f32[1,65,16,512]{3,1,2,0:T(8,128)S(1)}, f32[1,65,16,512]{...) fusion(f32[130,16,512]{2,0,1:T(8,128)S(1)} %copy-done.2, ...), kind=kLoop, calls=%fused_computation.40 | loop fusion | flops 9584640 | bytes 25567360 | tf_op jit(solution)/shard_map/stack | solution.py:114
  77.0 7.0 %fusion.21 = f32[2,65,16,512]{3,2,0,1:T(8,128)S(1)} fusion(f32[2,65,16,512,1]{3,1,2,0,4:T(8,128)S(1)} %maximum_bitcast_fusion, f32[1,16,2,16]{3,1,2,0:T(8,128)S(1)} %copy-done.25, f32[1,16,2,16]{3,1,2,0:T(8,128)S(1)} %copy-done.26), kind=kOutput, calls=%fused_computation.45 | convolution fusion | flops 408945664 | bytes 8523776 | tf_op jit(solution)/shard_map/sqrp,rkpc->skqc/dot_general | solution.py:18
  84.0 7.2 %fusion.27 = f32[2,65,16,512]{3,2,0,1:T(8,128)S(1)} fusion(f32[2,65,16,512,1]{3,1,2,0,4:T(8,128)S(1)} %maximum_bitcast_fusion.2, f32[1,16,2,16]{3,1,2,0:T(8,128)S(1)} %copy-done.25, f32[1,16,2,16]{3,1,2,0:T(8,128)S(1)} %copy-done.26), kind=kOutput, calls=%fused_computation.47 | convolution fusion | flops 408945664 | bytes 8523776 | tf_op jit(solution)/shard_map/sqrp,rkpc->skqc/dot_general | solution.py:18
  91.9 7.0 %fusion.24 = f32[2,65,16,512]{3,2,0,1:T(8,128)S(1)} fusion(f32[2,65,16,512,1]{3,1,2,0,4:T(8,128)S(1)} %maximum_bitcast_fusion.1, f32[1,16,2,16]{3,1,2,0:T(8,128)S(1)} %copy-done.25, f32[1,16,2,16]{3,1,2,0:T(8,128)S(1)} %copy-done.26), kind=kOutput, calls=%fused_computation.46 | convolution fusion | flops 408945664 | bytes 8523776 | tf_op jit(solution)/shard_map/sqrp,rkpc->skqc/dot_general | solution.py:18
  98.9 3.1 %multiply_subtract_fusion.3 = (f32[1,65,16,512]{3,2,0,1:T(8,128)}, f32[1,65,16,512]{3,2,0,1:T(8,128)}) fusion(f32[2,65,16,512]{3,2,0,1:T(8,128)S(1)} %fusion.27, f32[2,65,16,512]{3,2,0,1:T(8,128)S(1)} %fusion.21), kind=kLoop, calls=%fused_computation.58 | loop fusion | flops 3727360 | bytes 12779520 | tf_op jit(solution)/shard_map/sub | solution.py:156
  102.0 5.8 %multiply_subtract_fusion.1 = (f32[1,65,16,512]{3,2,0,1:T(8,128)}, f32[1,65,16,512]{3,2,0,1:T(8,128)}, f32[1,65,16,512]{3,2,0,1:T(8,128)}, f32[1,65,16,512]{3,2,0,1:T(8,128)}) fusion(f32[2,65,16,512]{3,2,0,1:T(8,128)S(1)} %fusion.27, f32[2,65,16,512]{3,2,0,1:T(8,128)S(1)} %fusion.24, f32[2,65,16,512]{3,2,0,1:T(8,128)S(1)} %fusion.21), kind=kLoop, calls=%fused_computation.54 | loop fusion | flops 6922240 | bytes 21299200 | tf_op jit(solution)/shard_map/sub | solution.py:156
  107.8 6.0 %fusion.32 = f32[2,65,16,512]{3,2,0,1:T(8,128)S(1)} fusion(f32[1,65,16,512]{3,2,0,1:T(8,128)} %get-tuple-element.56, f32[1,65,16,512]{3,2,0,1:T(8,128)} %get-tuple-element.57, f32[1,16,2,16]{3,1,2,0:T(8,128)S(1)} %copy-done.24, f32[1,16,2,16]{3,1,2,0:T(8,128)S(1)} %get-tuple-element.75), kind=kOutput, calls=%fused_computation.50 | convolution fusion | flops 410010624 | bytes 8523776 | tf_op jit(solution)/shard_map/sprq,rkqc->skpc/dot_general | solution.py:18
  113.8 4.5 %fusion.31 = f32[2,65,16,512]{3,2,0,1:T(8,128)S(1)} fusion(f32[1,65,16,512]{3,2,0,1:T(8,128)S(1)} %copy-done.13, f32[1,65,16,512]{3,2,0,1:T(8,128)S(1)} %copy-done.12, f32[1,16,2,16]{3,1,2,0:T(8,128)S(1)} %copy-done.24, f32[1,16,2,16]{3,1,2,0:T(8,128)S(1)} %get-tuple-element.75), kind=kOutput, calls=%fused_computation.49 | convolution fusion | flops 410010624 | bytes 8523776 | tf_op jit(solution)/shard_map/sprq,rkqc->skpc/dot_general | solution.py:18
  118.3 4.5 %fusion.30 = f32[2,65,16,512]{3,2,0,1:T(8,128)S(1)} fusion(f32[1,65,16,512]{3,2,0,1:T(8,128)S(1)} %copy-done.15, f32[1,65,16,512]{3,2,0,1:T(8,128)S(1)} %copy-done.14, f32[1,16,2,16]{3,1,2,0:T(8,128)S(1)} %copy-done.24, f32[1,16,2,16]{3,1,2,0:T(8,128)S(1)} %get-tuple-element.75), kind=kOutput, calls=%fused_computation.48 | convolution fusion | flops 410010624 | bytes 8523776 | tf_op jit(solution)/shard_map/sprq,rkqc->skpc/dot_general | solution.py:18
  122.8 4.4 %multiply_subtract_fusion = (f32[1,65,16,512]{3,2,0,1:T(8,128)}, f32[1,65,16,512]{3,2,0,1:T(8,128)}, f32[1,65,16,512]{3,2,0,1:T(8,128)S(1)}, f32[1,65,16,512]{3,...) fusion(f32[2,65,16,512]{3,2,0,1:T(8,128)S(1)} %fusion.30, f32[65,16]{1,0:T(8,128)S(1)} %copy-done.28, ...), kind=kLoop, calls=%fused_computation.52 | loop fusion | flops 9584640 | bytes 25567360 | tf_op jit(solution)/shard_map/sub | solution.py:139
  127.7 5.1 %fusion.56 = f32[64,16,512]{2,0,1:T(8,128)S(1)} fusion(f32[2,65,16,512]{3,2,0,1:T(8,128)S(1)} %pad_maximum_fusion.1, f32[64,1,65]{2,0,1:T(8,128)S(1)} %get-tuple-element.82, f32[64,1,65]{2,0,1:T(8,128)S(1)} %get-tuple-element.81), kind=kOutput, calls=%fused_computation.88 | convolution fusion | flops 817897600 | bytes 6390272 | tf_op jit(solution)/shard_map/nrk,rkpc->npc/dot_general | solution.py:18
  135.3 3.1 %copy.64 = f32[8,128,512]{1,2,0:T(8,128)} copy(f32[8,128,512]{2,1,0:T(8,128)} %bitcast.197) | data formatting | bytes 4194304 | tf_op jit(solution)/shard_map/reshape | solution.py:145
  140.7 5.1 %fusion.53 = f32[64,16,512]{2,0,1:T(8,128)S(1)} fusion(f32[2,65,16,512]{3,2,0,1:T(8,128)S(1)} %pad_maximum_fusion, f32[64,1,65]{2,0,1:T(8,128)S(1)} %get-tuple-element.82, f32[64,1,65]{2,0,1:T(8,128)S(1)} %get-tuple-element.81), kind=kOutput, calls=%fused_computation.87 | convolution fusion | flops 817897600 | bytes 6390272 | tf_op jit(solution)/shard_map/nrk,rkpc->npc/dot_general | solution.py:18
  148.3 3.0 %copy.57 = f32[8,128,512]{1,2,0:T(8,128)} copy(f32[8,128,512]{2,1,0:T(8,128)} %bitcast.198) | data formatting | bytes 4194304 | tf_op jit(solution)/shard_map/reshape | solution.py:145
  151.3 4.8 %fusion.44 = (f32[512]{0:T(512)}, bf16[8,128,512]{1,2,0:T(8,128)(2,1)}, bf16[8,128,512]{1,2,0:T(8,128)(2,1)S(1)}) fusion(bf16[128,8,512]{0,2,1:T(8,128)(2,1)} %all-to-all-done.2, bf16[128,8,512]{0,2,1:T(8,128)(2,1)S(1)} %copy-done.10, f32[8,128,512]{1,2,0:T(8,128)} %copy.57, f32[512]{0:T(512)S(1)} %bitcast.207, f32[8,128,512]{1,2,0:T(8,128)} %copy.64), kind=kLoop, calls=%fused_computation.74 | loop fusion | flops 5242368 | bytes 8392704 | tf_op jit(solution)/shard_map/reduce_sum | solution.py:199
  156.1 29.6 %all_to_all.46 = bf16[8,128,512]{1,2,0:T(8,128)(2,1)} all-to-all(bf16[8,128,512]{1,2,0:T(8,128)(2,1)S(1)} %get-tuple-element.62), channel_id=1, replica_groups=mesh['pipe'=4,'seq'=8] {'seq'}, dimensions={0} | all-to-all | bytes 2097152 | tf_op jit(solution)/shard_map/all_to_all | solution.py:206
  185.7 4.3 %all-to-all-start.1 = ((bf16[8,128,512]{1,2,0:T(8,128)(2,1)}), bf16[8,128,512]{1,2,0:T(8,128)(2,1)}, u32[]{:S(2)}, u32[]{:S(2)}) async-start(bf16[8,128,512]{1,2,0:T(8,128)(2,1)} %get-tuple-element.61), calls=%async_computation.1 | async-start | bytes 2097152 | tf_op jit(solution)/shard_map/all_to_all | solution.py:205
  190.0 4.4 %pad_maximum_fusion.2 = f32[2,65,16,512]{3,2,0,1:T(8,128)} fusion(f32[1,65,16,512]{3,2,0,1:T(8,128)} %get-tuple-element.51, f32[1,65,16,512]{3,2,0,1:T(8,128)S(1)} %copy-done.11), kind=kLoop, calls=%fused_computation.23 | loop fusion | flops 1064960 | bytes 8519680 | tf_op jit(solution)/shard_map/stack | solution.py:137
  197.9 17.2 %all-to-all-done.1 = bf16[8,128,512]{1,2,0:T(8,128)(2,1)} async-done(((bf16[8,128,512]{1,2,0:T(8,128)(2,1)}), bf16[8,128,512]{1,2,0:T(8,128)(2,1)}, u32[]{:S(2)}, u32[]{:S(2)}) %all-to-all-start.1) | async-done | bytes 1048608 | tf_op jit(solution)/shard_map/all_to_all | solution.py:205
  215.1 3.2 %fusion.41 = (bf16[128,4096]{0,1:T(8,128)(2,1)}, bf16[128,4096]{0,1:T(8,128)(2,1)}) fusion(bf16[1,128,4096]{1,2,0:T(8,128)(2,1)S(1)} %copy-done.4, bf16[8,128,512]{1,2,0:T(8,128)(2,1)} %all-to-all-done.1, bf16[1,128,4096]{1,2,0:T(8,128)(2,1)S(1)} %copy.45), kind=kLoop, calls=%fused_computation.71 | loop fusion | flops 3670016 | bytes 5242880 | tf_op jit(solution)/shard_map/convert_element_type | solution.py:223
  220.2 5.4 %multiply_multiply_fusion = (f32[64,16,512]{2,0,1:T(8,128)S(1)}, f32[64,16,512]{2,0,1:T(8,128)S(1)}) fusion(f32[64,16]{0,1:T(8,128)S(1)} %add_convert_fusion, f32[512]{0:T(512)S(1)} %bitcast.203, f32[2,65,16,512]{3,2,0,1:T(8,128)S(1)} %copy-done.1, f32[64,1,65]{2,0,1:T(8,128)S(1)} %get-tuple-element.82, f32[64,1,65]{2,0,1:T(8,128)S(1)} %get-tuple-element.81), kind=kOutput, calls=%fused_computation.84 | convolution fusion | flops 819994752 | bytes 8493568 | tf_op jit(solution)/shard_map/nrk,rkpc->npc/dot_general | solution.py:18
  229.4 2.9 %fusion.128 = (f32[64]{0:T(128)S(1)}, f32[1024,64]{0,1:T(8,128)S(1)}) fusion(f32[1024,64]{0,1:T(8,128)S(1)} %copy-done.21, f32[1024,512]{1,0:T(8,128)S(1)} %bitcast.196, f32[1,64,512]{2,1,0:T(8,128)S(1)} %copy-done), kind=kOutput, calls=%fused_computation.193 | convolution fusion | flops 402784192 | bytes 2752768 | tf_op jit(solution)/shard_map/fc,tc->ft/dot_general | solution.py:18
  232.6 35.9 %all-reduce = (f32[1,33,64]{2,1,0:T(8,128)S(1)}, f32[1,64]{1,0:T(1,128)}) all-reduce(f32[1,33,64]{2,1,0:T(8,128)S(1)} %convolution_bitcast_fusion.1, f32[1,64]{1,0:T(1,128)S(1)} %bitcast.206), channel_id=1, replica_groups=mesh['pipe'=4,'seq'=8] {'seq'}, use_global_device_ids=true, to_apply=%region_0.1 | all-reduce | flops 2176 | bytes 17408 | tf_op jit(solution)/shard_map/psum | solution.py:216
  269.2 2.9 %fusion.49 = (f32[512]{0:T(512)}, f32[1024,512]{1,0:T(8,128)S(1)}) fusion(f32[1024,512]{1,0:T(8,128)S(1)} %copy-done.17, f32[64,16,512]{2,1,0:T(8,128)} %copy.67, f32[1024]{0:T(1024)S(1)} %negate_multiply_fusion.1, f32[1024]{0:T(1024)S(1)} %copy-done.35, f32[512]{0:T(512)S(1)} %bitcast.204), kind=kLoop, calls=%fused_computation.81 | loop fusion | flops 3669504 | bytes 6303744 | tf_op jit(solution)/shard_map/reduce_sum | solution.py:210
  (126 shorter events, 50.1 us)
Async XLA Ops:
  0.6 45.2 %copy-start = (f32[1,64,512]{2,1,0:T(8,128)S(1)}, f32[1,64,512]{2,1,0:T(8,128)}, u32[]{:S(2)}) copy-start(f32[1,64,512]{2,1,0:T(8,128)} %param.15) | copy-start | bytes 393220
  3.1 8.6 %copy-start.36 = (f32[1,512]{1,0:T(1,128)S(1)}, f32[1,512]{1,0:T(1,128)}, u32[]{:S(2)}) copy-start(f32[1,512]{1,0:T(1,128)} %param.16) | copy-start | bytes 6148
  3.1 9.2 %copy-start.23 = (bf16[1,128,4096]{2,1,0:T(8,128)(2,1)S(1)}, bf16[1,128,4096]{2,1,0:T(8,128)(2,1)}, u32[]{:S(2)}) copy-start(bf16[1,128,4096]{2,1,0:T(8,128)(2,1)} %param.9) | copy-start | bytes 3145732
  4.4 33.2 %all-to-all-start.2 = ((bf16[128,8,512]{0,2,1:T(8,128)(2,1)}), bf16[128,8,512]{0,2,1:T(8,128)(2,1)}, u32[]{:S(2)}, u32[]{:S(2)}) async-start(bf16[128,8,512]{0,2,1:T(8,128)(2,1)} %bitcast.43), calls=%async_computation.2 | async-start | bytes 2097152 | tf_op jit(solution)/shard_map/all_to_all | solution.py:183
  12.9 7.6 %copy-start.5 = (bf16[1,128,4096]{1,2,0:T(8,128)(2,1)}, bf16[1,128,4096]{1,2,0:T(8,128)(2,1)S(1)}, u32[]{:S(2)}) copy-start(bf16[1,128,4096]{1,2,0:T(8,128)(2,1)S(1)} %copy.48) | copy-start | bytes 3145732
  14.9 22.6 %copy-start.7 = (bf16[1,128,4096]{1,2,0:T(8,128)(2,1)}, bf16[1,128,4096]{1,2,0:T(8,128)(2,1)S(1)}, u32[]{:S(2)}) copy-start(bf16[1,128,4096]{1,2,0:T(8,128)(2,1)S(1)} %copy.49) | copy-start | bytes 3145732
  15.0 3.4 %copy-start.29 = (f32[65,16]{0,1:T(8,128)}, f32[65,16]{0,1:T(8,128)S(1)}, u32[]{:S(2)}) copy-start(f32[65,16]{0,1:T(8,128)S(1)} %get-tuple-element.93) | copy-start | bytes 12484
  15.0 3.4 %copy-start.31 = (f32[65,16]{0,1:T(8,128)}, f32[65,16]{0,1:T(8,128)S(1)}, u32[]{:S(2)}) copy-start(f32[65,16]{0,1:T(8,128)S(1)} %get-tuple-element.94) | copy-start | bytes 12484
  37.5 29.7 %all-to-all-start = ((bf16[128,8,512]{0,2,1:T(8,128)(2,1)}), bf16[128,8,512]{0,2,1:T(8,128)(2,1)S(1)}, u32[]{:S(2)}, u32[]{:S(2)}) async-start(bf16[128,8,512]{0,2,1:T(8,128)(2,1)} %bitcast.199), calls=%async_computation | async-start | bytes 2097152 | tf_op jit(solution)/shard_map/all_to_all | solution.py:182
  48.7 6.2 %copy-start.16 = (f32[1024,512]{1,0:T(8,128)}, f32[1024,512]{1,0:T(8,128)S(1)}, u32[]{:S(2)}) copy-start(f32[1024,512]{1,0:T(8,128)S(1)} %fusion.52) | copy-start | bytes 6291460
  67.2 3.3 %copy-start.9 = (bf16[128,8,512]{0,2,1:T(8,128)(2,1)}, bf16[128,8,512]{0,2,1:T(8,128)(2,1)S(1)}, u32[]{:S(2)}) copy-start(bf16[128,8,512]{0,2,1:T(8,128)(2,1)S(1)} %all-to-all-done) | copy-start | bytes 3145732
  102.0 5.8 %copy-start.24 = (f32[1,16,2,16]{3,1,2,0:T(8,128)S(1)}, f32[1,16,2,16]{3,1,2,0:T(8,128)}, u32[]{:S(2)}) copy-start(f32[1,16,2,16]{3,1,2,0:T(8,128)} %get-tuple-element.80) | copy-start | bytes 6148
  107.8 6.0 %copy-start.12 = (f32[1,65,16,512]{3,2,0,1:T(8,128)S(1)}, f32[1,65,16,512]{3,2,0,1:T(8,128)}, u32[]{:S(2)}) copy-start(f32[1,65,16,512]{3,2,0,1:T(8,128)} %get-tuple-element.40) | copy-start | bytes 6389764
  107.8 6.0 %copy-start.13 = (f32[1,65,16,512]{3,2,0,1:T(8,128)S(1)}, f32[1,65,16,512]{3,2,0,1:T(8,128)}, u32[]{:S(2)}) copy-start(f32[1,65,16,512]{3,2,0,1:T(8,128)} %get-tuple-element.41) | copy-start | bytes 6389764
  113.8 4.5 %copy-start.14 = (f32[1,65,16,512]{3,2,0,1:T(8,128)S(1)}, f32[1,65,16,512]{3,2,0,1:T(8,128)}, u32[]{:S(2)}) copy-start(f32[1,65,16,512]{3,2,0,1:T(8,128)} %get-tuple-element.38) | copy-start | bytes 6389764
  113.8 4.5 %copy-start.15 = (f32[1,65,16,512]{3,2,0,1:T(8,128)S(1)}, f32[1,65,16,512]{3,2,0,1:T(8,128)}, u32[]{:S(2)}) copy-start(f32[1,65,16,512]{3,2,0,1:T(8,128)} %get-tuple-element.39) | copy-start | bytes 6389764
  118.3 4.5 %copy-start.27 = (f32[65,16]{1,0:T(8,128)S(1)}, f32[65,16]{1,0:T(8,128)}, u32[]{:S(2)}) copy-start(f32[65,16]{1,0:T(8,128)} %copy.53) | copy-start | bytes 12484
  118.3 4.5 %copy-start.28 = (f32[65,16]{1,0:T(8,128)S(1)}, f32[65,16]{1,0:T(8,128)}, u32[]{:S(2)}) copy-start(f32[65,16]{1,0:T(8,128)} %copy.54) | copy-start | bytes 12484
  156.1 33.9 %copy-start.11 = (f32[1,65,16,512]{3,2,0,1:T(8,128)S(1)}, f32[1,65,16,512]{3,2,0,1:T(8,128)}, u32[]{:S(2)}) copy-start(f32[1,65,16,512]{3,2,0,1:T(8,128)} %get-tuple-element.50) | copy-start | bytes 6389764
  185.7 29.4 %all-to-all-start.1 = ((bf16[8,128,512]{1,2,0:T(8,128)(2,1)}), bf16[8,128,512]{1,2,0:T(8,128)(2,1)}, u32[]{:S(2)}, u32[]{:S(2)}) async-start(bf16[8,128,512]{1,2,0:T(8,128)(2,1)} %get-tuple-element.61), calls=%async_computation.1 | async-start | bytes 2097152 | tf_op jit(solution)/shard_map/all_to_all | solution.py:205
  190.0 4.5 %copy-start.6 = (bf16[1,128,4096]{1,2,0:T(8,128)(2,1)S(1)}, bf16[1,128,4096]{1,2,0:T(8,128)(2,1)}, u32[]{:S(2)}) copy-start(bf16[1,128,4096]{1,2,0:T(8,128)(2,1)} %copy-done.5) | copy-start | bytes 3145732
  190.0 4.4 %copy-start.8 = (bf16[1,128,4096]{1,2,0:T(8,128)(2,1)S(1)}, bf16[1,128,4096]{1,2,0:T(8,128)(2,1)}, u32[]{:S(2)}) copy-start(bf16[1,128,4096]{1,2,0:T(8,128)(2,1)} %copy-done.7) | copy-start | bytes 3145732
  190.0 4.4 %copy-start.18 = (bf16[8,128,512]{1,2,0:T(8,128)(2,1)S(1)}, bf16[8,128,512]{1,2,0:T(8,128)(2,1)}, u32[]{:S(2)}) copy-start(bf16[8,128,512]{1,2,0:T(8,128)(2,1)} %all_to_all.46) | copy-start | bytes 3145732
  194.5 20.6 %copy-start.4 = (bf16[1,128,4096]{1,2,0:T(8,128)(2,1)S(1)}, bf16[1,128,4096]{1,2,0:T(8,128)(2,1)}, u32[]{:S(2)}) copy-start(bf16[1,128,4096]{1,2,0:T(8,128)(2,1)} %copy-done.3) | copy-start | bytes 3145732
  196.3 77.8 %collective-permute-start.1 = (bf16[128,4096]{0,1:T(8,128)(2,1)}, bf16[128,4096]{0,1:T(8,128)(2,1)}, u32[]{:S(2)}, u32[]{:S(2)}) collective-permute-start(bf16[128,4096]{0,1:T(8,128)(2,1)} %get-tuple-element.66), channel_id=1, source_target_pairs={{0,24},{8,0},{16,8},{24,16},{1,25},{9,1},{17,9},{25,17},{2,26},{10... | collective-permute-start | bytes 3145736 | tf_op jit(solution)/shard_map/ppermute | solution.py:14
  196.3 23.9 %copy-start.34 = (f32[1,512]{1,0:T(1,128)S(1)}, f32[1,512]{1,0:T(1,128)}, u32[]{:S(2)}) copy-start(f32[1,512]{1,0:T(1,128)} %neg.49) | copy-start | bytes 6148
  196.3 80.1 %collective-permute-start.2 = (bf16[128,4096]{0,1:T(8,128)(2,1)}, bf16[128,4096]{0,1:T(8,128)(2,1)}, u32[]{:S(2)}, u32[]{:S(2)}) collective-permute-start(bf16[128,4096]{0,1:T(8,128)(2,1)} %get-tuple-element.65), channel_id=1, source_target_pairs={{0,24},{8,0},{16,8},{24,16},{1,25},{9,1},{17,9},{25,17},{2,26},{10... | collective-permute-start | bytes 3145736 | tf_op jit(solution)/shard_map/ppermute | solution.py:14
  215.1 5.1 %copy-start.1 = (f32[2,65,16,512]{3,2,0,1:T(8,128)S(1)}, f32[2,65,16,512]{3,2,0,1:T(8,128)}, u32[]{:S(2)}) copy-start(f32[2,65,16,512]{3,2,0,1:T(8,128)} %pad_maximum_fusion.2) | copy-start | bytes 12779524
  218.3 60.3 %collective-permute-start = (bf16[128,4096]{0,1:T(8,128)(2,1)}, bf16[128,4096]{0,1:T(8,128)(2,1)}, u32[]{:S(2)}, u32[]{:S(2)}) collective-permute-start(bf16[128,4096]{0,1:T(8,128)(2,1)} %get-tuple-element.64), channel_id=1, source_target_pairs={{0,8},{8,16},{16,24},{24,0},{1,9},{9,17},{17,25},{25,1},{2,10},{10... | collective-permute-start | bytes 3145736 | tf_op jit(solution)/shard_map/ppermute | solution.py:14
  218.3 62.6 %collective-permute-start.3 = (bf16[128,4096]{0,1:T(8,128)(2,1)}, bf16[128,4096]{0,1:T(8,128)(2,1)}, u32[]{:S(2)}, u32[]{:S(2)}) collective-permute-start(bf16[128,4096]{0,1:T(8,128)(2,1)} %get-tuple-element.63), channel_id=1, source_target_pairs={{0,24},{8,0},{16,8},{24,16},{1,25},{9,1},{17,9},{25,17},{2,26},{10... | collective-permute-start | bytes 3145736 | tf_op jit(solution)/shard_map/ppermute | solution.py:14
  229.4 39.8 %copy-start.17 = (f32[1024,512]{1,0:T(8,128)S(1)}, f32[1024,512]{1,0:T(8,128)}, u32[]{:S(2)}) copy-start(f32[1024,512]{1,0:T(8,128)} %copy-done.16) | copy-start | bytes 6291460
  229.4 39.8 %copy-start.35 = (f32[1024]{0:T(1024)S(1)}, f32[1024]{0:T(1024)}, u32[]{:S(2)}) copy-start(f32[1024]{0:T(1024)} %iota_convert_fusion) | copy-start | bytes 12292
  (13 other events, 26.7 us)
where the time goes:
time: 287 us; the launch traced here: 283 us
  matrix products  76.1 us (27%)
  blocking collectives  65.5 us (23%)
  other arithmetic  47 us (16%)
  waiting for transfers between devices  40.2 us (14%)
  local copies, waits for them, and re-layouts  34.3 us (12%)
  starting transfers between devices  18.9 us (7%)
    dot_general x17, matrix products, contract(): return jnp.einsum(form, left, right, precision=lax.Precision.HIGHEST)  76.1 us
    psum x1, blocking collectives, per_device(): grad_embed_w, grad_embed_b = lax.psum((part_weight, part_bias), 'seq')  35.9 us
    all_to_all x1, blocking collectives, per_device(): lax.all_to_all(grad_chan, 'seq', split_axis=0, concat_axis=1, tiled=True)  29.6 us
    all_to_all x1, waiting for transfers between devices, per_device(): lax.all_to_all(mixed_chan, 'seq', split_axis=0, concat_axis=1, tiled=True)  17.2 us
    all_to_all x1, waiting for transfers between devices, per_device(): lax.all_to_all(upstream, 'seq', split_axis=1, concat_axis=0, tiled=True)  17 us
    unnamed x85, local copies, waits for them, and re-layouts  15.7 us
    sub x2, other arithmetic, spectral_product(): left_re * right_re - left_im * right_im  8.87 us
    dot_general x3, local copies, waits for them, and re-layouts, contract(): return jnp.einsum(form, left, right, precision=lax.Precision.HIGHEST)  7.63 us
  transfers between devices with their start and end apart: 7, of which 3 were waited for; matrix products, arithmetic and copies ran while one was open for 22% of the time, Pallas kernels for 0%

commit v1 on v0

--- a/solution.py
+++ b/solution.py
@@ -94,7 +94,7 @@
     )
 
 
-def forward_transform(field, tables_all):
+def staged_forward(field, tables_all):
     (
         table_first,
         cos_twist,
@@ -118,7 +118,7 @@
     return contract("sqrp,rkpc->skqc", table_second, twisted)
 
 
-def inverse_transform(spec, tables_all):
+def staged_inverse(spec, tables_all):
     (
         table_first,
         cos_twist,
@@ -145,6 +145,46 @@
     return result.reshape(half_len * inner_len, columns)
 
 
+def dense_tables(length):
+    block = 128
+    fine = jnp.arange(block, dtype=jnp.int32)
+    coarse = jnp.arange(length // block, dtype=jnp.int32) * block
+    point = jnp.arange(length, dtype=jnp.int32)
+    unit = math.pi / (2 * length)
+
+    def pair(count):
+        angle = unit * (count % (4 * length)).astype(jnp.float32)
+        return jnp.cos(angle), jnp.sin(angle)
+
+    def joined(first, second):
+        (cos_f, sin_f), (cos_s, sin_s) = first, second
+        cos_j = cos_s[:, None, :] * cos_f[None] - sin_s[:, None, :] * sin_f[None]
+        sin_j = sin_s[:, None, :] * cos_f[None] + cos_s[:, None, :] * sin_f[None]
+        return cos_j.reshape(length, length), sin_j.reshape(length, length)
+
+    odd = 2 * point + 1
+    cos_k, sin_k = joined(
+        pair((2 * fine + 1)[:, None] * point[None, :]),
+        pair((2 * coarse)[:, None] * point[None, :]),
+    )
+    ahead = jnp.concatenate([cos_k, -sin_k], axis=0).astype(jnp.bfloat16)
+    cos_n, sin_n = joined(
+        pair(fine[:, None] * odd[None, :]), pair(coarse[:, None] * odd[None, :])
+    )
+    back = (jnp.concatenate([cos_n, -sin_n], axis=1) * (1.0 / length)).astype(jnp.bfloat16)
+    return ahead, back
+
+
+def dense_forward(field, tables_all):
+    spec = jnp.dot(tables_all[0], field.astype(jnp.bfloat16), preferred_element_type=jnp.float32)
+    return spec.reshape(2, field.shape[0], field.shape[1])
+
+
+def dense_inverse(spec, tables_all):
+    flat = spec.reshape(2 * spec.shape[1], spec.shape[2])
+    return jnp.dot(tables_all[1], flat.astype(jnp.bfloat16), preferred_element_type=jnp.float32)
+
+
 def spectral_product(left, right, conjugate_left):
     left_re = left[0]
     left_im = left[1]
@@ -175,7 +215,12 @@
     positions = jnp.arange(length, dtype=jnp.int32).astype(jnp.float32)[:, None]
     envelope = jnp.exp(-decay[0][None, :] * positions / length) * (1.0 / math.sqrt(length))
     kernel = contract("ft,fc->tc", activation, filter_w) * envelope
-    tables_all = build_tables(length)
+    if length <= 1024 and length % 128 == 0:
+        tables_all = dense_tables(length)
+        forward_transform, inverse_transform = dense_forward, dense_inverse
+    else:
+        tables_all = build_tables(length)
+        forward_transform, inverse_transform = staged_forward, staged_inverse
     kernel_spec = forward_transform(kernel, tables_all)
     skip_row = skip[0][None, :]
     weighted_chan, upstream_chan = (

time: 287 us -> 204 us (0.71)
  matrix products: 76.1 us -> 37.4 us
  blocking collectives: 65.5 us -> 35.7 us
  waiting for transfers between devices: 40.2 us -> 59.8 us
  other arithmetic: 47 us -> 28.9 us
  local copies, waits for them, and re-layouts: 34.3 us -> 19.6 us
    dot_general x17 -> x5, matrix products: 76.1 us -> 12.5 us  [contract(): return jnp.einsum(form, left, right, precision=lax.Precision.HIGHEST)]
    all_to_all x1 -> x0, blocking collectives: 29.6 us -> none  [per_device(): lax.all_to_all(grad_chan, 'seq', split_axis=0, concat_axis=1, tiled=True)]
    dot_general x0 -> x6, matrix products: none -> 24.8 us  [the longest x3 13.8 us: dense_forward(): jnp.dot(tables_all[0], field.astype(jnp.bfloat16), preferred_element_type...]
    all_to_all x0 -> x1, waiting for transfers between devices: none -> 22.3 us  [per_device(): lax.all_to_all(grad_chan, 'seq', split_axis=0, concat_axis=1, tiled=True)]
    sub x3 -> x1, other arithmetic: 13.3 us -> 4.47 us  [joined(): cos_j = cos_s[:, None, :] * cos_f[None] - sin_s[:, None, :] * sin_f[None]]
    dot_general x3 -> x0, local copies, waits for them, and re-layouts: 7.63 us -> none  [contract(): return jnp.einsum(form, left, right, precision=lax.Precision.HIGHEST)]
    reshape x2 -> x0, local copies, waits for them, and re-layouts: 6.1 us -> none  [inverse_transform(): return result.reshape(half_len * inner_len, columns)]
    cos x0 -> x4, other arithmetic: none -> 5.68 us  [pair(): return (jnp.cos(angle), jnp.sin(angle))]
  transfers between devices with their start and end apart: 7 -> 8, of which waited for: 3 -> 4; matrix products, arithmetic and copies ran while one was open for 22% -> 26% of each run, Pallas kernels for 0% -> 0%
where the time goes in v1:
time: 204 us; the launch traced here: 203 us
  waiting for transfers between devices  59.8 us (29%)
  matrix products  37.4 us (18%)
  blocking collectives  35.7 us (18%)
  other arithmetic  28.9 us (14%)
  starting transfers between devices  20.5 us (10%)
  local copies, waits for them, and re-layouts  19.6 us (10%)
    psum x1, blocking collectives, per_device(): grad_embed_w, grad_embed_b = lax.psum((part_weight, part_bias), 'seq')  35.7 us
    all_to_all x1, waiting for transfers between devices, per_device(): lax.all_to_all(grad_chan, 'seq', split_axis=0, concat_axis=1, tiled=True)  22.3 us
    unnamed x65, local copies, waits for them, and re-layouts  16.6 us
    all_to_all x1, waiting for transfers between devices, per_device(): lax.all_to_all(mixed_chan, 'seq', split_axis=0, concat_axis=1, tiled=True)  15.5 us
    dot_general x3, matrix products, dense_forward(): jnp.dot(tables_all[0], field.astype(jnp.bfloat16), preferred_element_type...  13.8 us
    dot_general x5, matrix products, contract(): return jnp.einsum(form, left, right, precision=lax.Precision.HIGHEST)  12.5 us
    all_to_all x1, waiting for transfers between devices, per_device(): lax.all_to_all(upstream, 'seq', split_axis=1, concat_axis=0, tiled=True)  11.9 us
    dot_general x3, matrix products, dense_inverse(): jnp.dot(tables_all[1], flat.astype(jnp.bfloat16), preferred_element_type=...  11 us
  transfers between devices with their start and end apart: 8, of which 4 were waited for; matrix products, arithmetic and copies ran while one was open for 26% of the time, Pallas kernels for 0%

profile of v1, /device:TPU:0, one launch (start us, length us, event | category | flops | bytes accessed | tf_op | source)
XLA Modules:
  0.0 202.9 jit_solution(786132404300499328)
XLA Ops:
  0.7 1.8 fusion.10
  4.2 7.3 %all-to-all-start.2 = ((bf16[128,8,512]{2,0,1:T(8,128)(2,1)}), bf16[128,8,512]{2,0,1:T(8,128)(2,1)S(1)}, u32[]{:S(2)}, u32[]{:S(2)}) async-start(bf16[128,8,512]{2,0,1:T(8,128)(2,1)} %copy.20), calls=%async_computation.2 | async-start | bytes 2097152 | tf_op jit(solution)/shard_map/all_to_all | solution.py:228
  14.7 1.9 fusion.95
  16.6 3.2 %fusion.54 = (f32[128,1024]{1,0:T(8,128)}, f32[128,1024]{1,0:T(8,128)}) fusion(s32[128]{0:T(128)S(1)} %multiply_add_fusion.1), kind=kLoop, calls=%fused_computation.84 | loop fusion | flops 1835008 | bytes 1049088 | tf_op jit(solution)/shard_map/cos | solution.py:157
  19.8 2.0 %fusion.56 = (f32[128,1024]{1,0:T(8,128)S(1)}, f32[128,1024]{1,0:T(8,128)S(1)}) fusion(s32[1024]{0:T(1024)S(1)} %multiply_add_fusion), kind=kLoop, calls=%fused_computation.86 | loop fusion | flops 1835008 | bytes 1052672 | tf_op jit(solution)/shard_map/cos | solution.py:157
  21.8 3.5 %fusion.12 = f32[1024,512]{1,0:T(8,128)} fusion(f32[1024,64]{0,1:T(8,128)S(1)} %get-tuple-element.46, f32[1024]{0:T(1024)S(1)} %iota_convert_fusion, f32[512]{0:T(512)S(1)} %bitcast.129, f32[1,64,512]{2,1,0:T(8,128)S(1)} %copy-done), kind=kOutput, calls=%fused_computation.40 | convolution fusion | flops 404750336 | bytes 2496512 | tf_op jit(solution)/shard_map/ft,fc->tc/dot_general | solution.py:18
  25.3 11.9 %all-to-all-done.2 = bf16[128,8,512]{2,0,1:T(8,128)(2,1)S(1)} async-done(((bf16[128,8,512]{2,0,1:T(8,128)(2,1)}), bf16[128,8,512]{2,0,1:T(8,128)(2,1)S(1)}, u32[]{:S(2)}, u32[]{:S(2)}) %all-to-all-start.2) | async-done | bytes 1048608 | tf_op jit(solution)/shard_map/all_to_all | solution.py:228
  37.2 3.7 %all-to-all-start = ((bf16[128,8,512]{2,0,1:T(8,128)(2,1)}), bf16[128,8,512]{2,0,1:T(8,128)(2,1)S(1)}, u32[]{:S(2)}, u32[]{:S(2)}) async-start(bf16[128,8,512]{2,0,1:T(8,128)(2,1)} %copy.18), calls=%async_computation | async-start | bytes 2097152 | tf_op jit(solution)/shard_map/all_to_all | solution.py:227
  41.0 2.4 %subtract_convert_fusion = (bf16[8,128,1024]{2,1,0:T(8,128)(2,1)S(1)}, bf16[8,128,1024]{2,1,0:T(8,128)(2,1)S(1)}) fusion(f32[128,1024]{1,0:T(8,128)} %get-tuple-element.45, f32[8,1024]{1,0:T(8,128)S(1)} %get-tuple-element.43, f32[128,1024]{1,0:T(8,128)} %get-tuple-element.44, f32[8,1024]{1,0:T(8,128)S(1)} %get-tuple-element.42), kind=kLoop, calls=%fused_computation.4 | loop fusion | flops 9437184 | bytes 5308416 | tf_op jit(solution)/shard_map/convert.23
  43.5 4.5 %multiply_subtract_fusion = (f32[8,128,1024]{2,1,0:T(8,128)}, f32[8,128,1024]{2,1,0:T(8,128)}) fusion(f32[128,1024]{1,0:T(8,128)S(1)} %get-tuple-element.39, f32[8,1024]{1,0:T(8,128)S(1)} %get-tuple-element.37, f32[128,1024]{1,0:T(8,128)S(1)} %get-tuple-element.38, f32[8,1024]{1,0:T(8,128)S(1)} %get-tuple-element.36), kind=kLoop, calls=%fused_computation.6 | loop fusion | flops 7340032 | bytes 9502720 | tf_op jit(solution)/shard_map/sub | solution.py:161
  47.9 4.4 %fusion.19 = f32[2048,512]{1,0:T(8,128)} fusion(bf16[1024,1024]{1,0:T(8,128)(2,1)S(1)} %bitcast.122, bf16[1024,1024]{1,0:T(8,128)(2,1)S(1)} %bitcast.119, f32[1024,512]{1,0:T(8,128)S(1)} %copy-done.28), kind=kOutput, calls=%fused_computation.45 | convolution fusion | flops 2156396544 | bytes 10485760 | tf_op jit(solution)/shard_map/dot_general | solution.py:179
  52.3 4.5 %fusion.17 = f32[2048,512]{1,0:T(8,128)} fusion(bf16[1024,512]{1,0:T(8,128)(2,1)S(1)} %bitcast.111, bf16[1024,1024]{1,0:T(8,128)(2,1)S(1)} %bitcast.123, bf16[1024,1024]{1,0:T(8,128)(2,1)S(1)} %bitcast.120), kind=kOutput, calls=%fused_computation.43 | convolution fusion | flops 2155872256 | bytes 9437184 | tf_op jit(solution)/shard_map/dot_general | solution.py:179
  56.8 10.1 %all-to-all-done = bf16[128,8,512]{2,0,1:T(8,128)(2,1)S(1)} async-done(((bf16[128,8,512]{2,0,1:T(8,128)(2,1)}), bf16[128,8,512]{2,0,1:T(8,128)(2,1)S(1)}, u32[]{:S(2)}, u32[]{:S(2)}) %all-to-all-start) | async-done | bytes 1048608 | tf_op jit(solution)/shard_map/all_to_all | solution.py:227
  66.8 5.0 %fusion.18 = f32[2048,512]{1,0:T(8,128)S(1)} fusion(bf16[1024,512]{1,0:T(8,128)(2,1)S(1)} %bitcast.113, bf16[1024,1024]{1,0:T(8,128)(2,1)} %bitcast.124, bf16[1024,1024]{1,0:T(8,128)(2,1)} %bitcast.121), kind=kOutput, calls=%fused_computation.44 | convolution fusion | flops 2155872256 | bytes 9437184 | tf_op jit(solution)/shard_map/dot_general | solution.py:179
  71.9 1.9 fusion.30
  78.1 3.3 %add_convert_fusion.3 = bf16[1024,512]{1,0:T(8,128)(2,1)} fusion(bf16[1024,512]{1,0:T(8,128)(2,1)S(1)} %bitcast.114, bf16[2048,512]{1,0:T(8,128)(2,1)S(1)} %bitcast.125, f32[512]{0:T(512)S(1)} %bitcast.134, f32[1024,1024]{1,0:T(8,128)S(1)} %bitcast.106, f32[1024,1024]{1,0:T(8,128)S(1)} %bitcast.103), kind=kOutput, calls=%fused_computation.35 | convolution fusion | flops 2155872256 | bytes 12584960 | tf_op jit(solution)/shard_map/dot_general | solution.py:185
  81.4 3.8 %all-to-all-start.1 = ((bf16[8,128,512]{2,1,0:T(8,128)(2,1)}), bf16[8,128,512]{2,1,0:T(8,128)(2,1)S(1)}, u32[]{:S(2)}, u32[]{:S(2)}) async-start(bf16[8,128,512]{2,1,0:T(8,128)(2,1)} %bitcast.15), calls=%async_computation.1 | async-start | bytes 2097152 | tf_op jit(solution)/shard_map/all_to_all | solution.py:250
  85.2 4.8 %fusion.28 = (bf16[1,1024,512]{2,1,0:T(8,128)(2,1)S(1)}, bf16[1,1024,512]{2,1,0:T(8,128)(2,1)S(1)}) fusion(f32[2048,512]{1,0:T(8,128)} %fusion.17, f32[2048,512]{1,0:T(8,128)} %fusion.19), kind=kLoop, calls=%fused_computation.52 | loop fusion | flops 4718592 | bytes 10485760 | tf_op jit(solution)/shard_map/stack | solution.py:195
  90.2 2.0 copy-done.4
  92.2 3.3 %add_convert_fusion.1 = bf16[1024,512]{1,0:T(8,128)(2,1)} fusion(bf16[1024,512]{1,0:T(8,128)(2,1)S(1)} %bitcast.112, bf16[2048,512]{1,0:T(8,128)(2,1)S(1)} %bitcast.117, f32[512]{0:T(512)S(1)} %bitcast.135, f32[1024,1024]{1,0:T(8,128)S(1)} %bitcast.107, f32[1024,1024]{1,0:T(8,128)S(1)} %bitcast.104), kind=kOutput, calls=%fused_computation.32 | convolution fusion | flops 2155872256 | bytes 12584960 | tf_op jit(solution)/shard_map/dot_general | solution.py:185
  95.5 15.5 %all-to-all-done.1 = bf16[8,128,512]{2,1,0:T(8,128)(2,1)S(1)} async-done(((bf16[8,128,512]{2,1,0:T(8,128)(2,1)}), bf16[8,128,512]{2,1,0:T(8,128)(2,1)S(1)}, u32[]{:S(2)}, u32[]{:S(2)}) %all-to-all-start.1) | async-done | bytes 1048608 | tf_op jit(solution)/shard_map/all_to_all | solution.py:250
  111.0 3.6 %all-to-all-start.3 = ((bf16[8,128,512]{2,1,0:T(8,128)(2,1)}), bf16[8,128,512]{2,1,0:T(8,128)(2,1)S(1)}, u32[]{:S(2)}, u32[]{:S(2)}) async-start(bf16[8,128,512]{2,1,0:T(8,128)(2,1)} %bitcast.127), calls=%async_computation.3 | async-start | bytes 2097152 | tf_op jit(solution)/shard_map/all_to_all | solution.py:251
  116.4 1.9 fusion.7
  118.3 22.3 %all-to-all-done.3 = bf16[8,128,512]{2,1,0:T(8,128)(2,1)S(1)} async-done(((bf16[8,128,512]{2,1,0:T(8,128)(2,1)}), bf16[8,128,512]{2,1,0:T(8,128)(2,1)S(1)}, u32[]{:S(2)}, u32[]{:S(2)}) %all-to-all-start.3) | async-done | bytes 1048608 | tf_op jit(solution)/shard_map/all_to_all | solution.py:251
  142.1 1.9 fusion.2
  146.1 4.4 %multiply_reduce_fusion.1 = (f32[512]{0:T(512)}, f32[1024,512]{1,0:T(8,128)S(1)}) fusion(f32[1024,512]{1,0:T(8,128)} %fusion.12, f32[1024]{0:T(1024)S(1)} %negate_multiply_fusion, bf16[2048,512]{1,0:T(8,128)(2,1)S(1)} %bitcast.118, f32[1024,1024]{1,0:T(8,128)S(1)} %bitcast.108, f32[1024,1024]{1,0:T(8,128)S(1)} %bitcast.105), kind=kOutput, calls=%fused_computation.29 | convolution fusion | flops 2155347456 | bytes 14686208 | tf_op jit(solution)/shard_map/dot_general | solution.py:185
  150.5 3.3 %fusion.96 = (f32[64]{0:T(128)S(1)}, f32[1024,64]{0,1:T(8,128)S(1)}) fusion(f32[1024,64]{0,1:T(8,128)S(1)} %copy-done.21, f32[1,64,512]{2,1,0:T(8,128)S(1)} %copy-done, f32[1024,512]{1,0:T(8,128)S(1)} %get-tuple-element.51, f32[1024]{0:T(1024)S(1)} %iota_convert_fusion, f32[512]{0:T(512)S(1)} %bitcast.130), kind=kOutput, calls=%fused_computation.143 | convolution fusion | flops 404881344 | bytes 2758912 | tf_op jit(solution)/shard_map/fc,tc->ft/dot_general | solution.py:18
  154.2 35.7 %all-reduce = (f32[1,33,64]{2,1,0:T(8,128)S(1)}, f32[1,64]{1,0:T(1,128)}) all-reduce(f32[1,33,64]{2,1,0:T(8,128)S(1)} %convolution_bitcast_fusion, f32[1,64]{1,0:T(1,128)S(1)} %bitcast.133), channel_id=1, replica_groups=mesh['pipe'=4,'seq'=8] {'seq'}, use_global_device_ids=true, to_apply=%region_0.1 | all-reduce | flops 2176 | bytes 17408 | tf_op jit(solution)/shard_map/psum | solution.py:261
  191.5 3.4 %fusion.23 = f32[1,64,512]{2,1,0:T(8,128)} fusion(f32[1024,64]{0,1:T(8,128)} %copy-done.20, f32[1024,512]{1,0:T(8,128)S(1)} %copy-done.27, f32[1024]{0:T(1024)S(1)} %iota_convert_fusion, f32[512]{0:T(512)S(1)} %bitcast.131), kind=kOutput, calls=%fused_computation.48 | convolution fusion | flops 404750336 | bytes 2496512 | tf_op jit(solution)/shard_map/ft,tc->fc/dot_general | solution.py:18
  195.0 2.3 %copy.38 = bf16[1,128,4096]{2,1,0:T(8,128)(2,1)} copy(bf16[1,128,4096]{2,1,0:T(8,128)(2,1)} %bitcast.17) | data formatting | bytes 2097152
  197.3 2.3 %copy.39 = bf16[1,128,4096]{2,1,0:T(8,128)(2,1)} copy(bf16[1,128,4096]{2,1,0:T(8,128)(2,1)} %bitcast.27) | data formatting | bytes 2097152
  200.6 2.3 %copy.41 = bf16[1,128,4096]{2,1,0:T(8,128)(2,1)} copy(bf16[1,128,4096]{2,1,0:T(8,128)(2,1)} %bitcast.31) | data formatting | bytes 2097152
  (92 shorter events, 17.7 us)
Async XLA Ops:
  0.6 21.2 %copy-start = (f32[1,64,512]{2,1,0:T(8,128)S(1)}, f32[1,64,512]{2,1,0:T(8,128)}, u32[]{:S(2)}) copy-start(f32[1,64,512]{2,1,0:T(8,128)} %param.15) | copy-start | bytes 393220
  2.9 8.6 %copy-start.13 = (bf16[1,128,4096]{2,1,0:T(8,128)(2,1)S(1)}, bf16[1,128,4096]{2,1,0:T(8,128)(2,1)}, u32[]{:S(2)}) copy-start(bf16[1,128,4096]{2,1,0:T(8,128)(2,1)} %param.10) | copy-start | bytes 3145732
  2.9 8.6 %copy-start.15 = (bf16[1,128,4096]{2,1,0:T(8,128)(2,1)S(1)}, bf16[1,128,4096]{2,1,0:T(8,128)(2,1)}, u32[]{:S(2)}) copy-start(bf16[1,128,4096]{2,1,0:T(8,128)(2,1)} %param.9) | copy-start | bytes 3145732
  4.2 33.0 %all-to-all-start.2 = ((bf16[128,8,512]{2,0,1:T(8,128)(2,1)}), bf16[128,8,512]{2,0,1:T(8,128)(2,1)S(1)}, u32[]{:S(2)}, u32[]{:S(2)}) async-start(bf16[128,8,512]{2,0,1:T(8,128)(2,1)} %copy.20), calls=%async_computation.2 | async-start | bytes 2097152 | tf_op jit(solution)/shard_map/all_to_all | solution.py:228
  12.2 2.5 %copy-start.22 = (f32[1,33,64]{2,0,1:T(1,128)S(1)}, f32[1,33,64]{2,0,1:T(1,128)}, u32[]{:S(2)}) copy-start(f32[1,33,64]{2,0,1:T(1,128)} %param.13) | copy-start | bytes 25348
  12.2 2.5 %copy-start.24 = (f32[1,64]{1,0:T(1,128)S(1)}, f32[1,64]{1,0:T(1,128)}, u32[]{:S(2)}) copy-start(f32[1,64]{1,0:T(1,128)} %param.14) | copy-start | bytes 772
  16.6 5.3 %copy-start.20 = (f32[1024,64]{0,1:T(8,128)}, f32[1024,64]{0,1:T(8,128)S(1)}, u32[]{:S(2)}) copy-start(f32[1024,64]{0,1:T(8,128)S(1)} %get-tuple-element.46) | copy-start | bytes 786436
  37.2 29.6 %all-to-all-start = ((bf16[128,8,512]{2,0,1:T(8,128)(2,1)}), bf16[128,8,512]{2,0,1:T(8,128)(2,1)S(1)}, u32[]{:S(2)}, u32[]{:S(2)}) async-start(bf16[128,8,512]{2,0,1:T(8,128)(2,1)} %copy.18), calls=%async_computation | async-start | bytes 2097152 | tf_op jit(solution)/shard_map/all_to_all | solution.py:227
  43.4 8.9 %copy-start.18 = (bf16[8,128,1024]{2,1,0:T(8,128)(2,1)}, bf16[8,128,1024]{2,1,0:T(8,128)(2,1)S(1)}, u32[]{:S(2)}) copy-start(bf16[8,128,1024]{2,1,0:T(8,128)(2,1)S(1)} %get-tuple-element.34) | copy-start | bytes 6291460
  43.4 8.9 %copy-start.19 = (bf16[8,128,1024]{2,1,0:T(8,128)(2,1)}, bf16[8,128,1024]{2,1,0:T(8,128)(2,1)S(1)}, u32[]{:S(2)}) copy-start(bf16[8,128,1024]{2,1,0:T(8,128)(2,1)S(1)} %get-tuple-element.35) | copy-start | bytes 6291460
  43.4 4.5 %copy-start.28 = (f32[1024,512]{1,0:T(8,128)S(1)}, f32[1024,512]{1,0:T(8,128)}, u32[]{:S(2)}) copy-start(f32[1024,512]{1,0:T(8,128)} %fusion.12) | copy-start | bytes 6291460
  66.8 8.8 %copy-start.9 = (bf16[128,8,512]{2,0,1:T(8,128)(2,1)}, bf16[128,8,512]{2,0,1:T(8,128)(2,1)S(1)}, u32[]{:S(2)}) copy-start(bf16[128,8,512]{2,0,1:T(8,128)(2,1)S(1)} %all-to-all-done) | copy-start | bytes 3145732
  66.8 5.0 %copy-start.1 = (f32[2048,512]{1,0:T(8,128)S(1)}, f32[2048,512]{1,0:T(8,128)}, u32[]{:S(2)}) copy-start(f32[2048,512]{1,0:T(8,128)} %fusion.19) | copy-start | bytes 12582916
  66.8 5.1 %copy-start.2 = (f32[2048,512]{1,0:T(8,128)S(1)}, f32[2048,512]{1,0:T(8,128)}, u32[]{:S(2)}) copy-start(f32[2048,512]{1,0:T(8,128)} %fusion.17) | copy-start | bytes 12582916
  73.9 2.9 %copy-start.3 = (f32[8,128,1024]{2,1,0:T(8,128)S(1)}, f32[8,128,1024]{2,1,0:T(8,128)}, u32[]{:S(2)}) copy-start(f32[8,128,1024]{2,1,0:T(8,128)} %get-tuple-element.32) | copy-start | bytes 12582916
  73.9 4.2 %copy-start.6 = (f32[8,128,1024]{2,1,0:T(8,128)S(1)}, f32[8,128,1024]{2,1,0:T(8,128)}, u32[]{:S(2)}) copy-start(f32[8,128,1024]{2,1,0:T(8,128)} %get-tuple-element.33) | copy-start | bytes 12582916
  73.9 4.2 %copy-start.25 = (f32[1,512]{1,0:T(1,128)S(1)}, f32[1,512]{1,0:T(1,128)}, u32[]{:S(2)}) copy-start(f32[1,512]{1,0:T(1,128)} %param.17) | copy-start | bytes 6148
  81.4 29.6 %all-to-all-start.1 = ((bf16[8,128,512]{2,1,0:T(8,128)(2,1)}), bf16[8,128,512]{2,1,0:T(8,128)(2,1)S(1)}, u32[]{:S(2)}, u32[]{:S(2)}) async-start(bf16[8,128,512]{2,1,0:T(8,128)(2,1)} %bitcast.15), calls=%async_computation.1 | async-start | bytes 2097152 | tf_op jit(solution)/shard_map/all_to_all | solution.py:250
  85.2 5.0 %copy-start.7 = (f32[8,128,1024]{2,1,0:T(8,128)S(1)}, f32[8,128,1024]{2,1,0:T(8,128)}, u32[]{:S(2)}) copy-start(f32[8,128,1024]{2,1,0:T(8,128)} %get-tuple-element.33) | copy-start | bytes 12582916
  90.0 2.2 %copy-start.4 = (f32[8,128,1024]{2,1,0:T(8,128)S(1)}, f32[8,128,1024]{2,1,0:T(8,128)}, u32[]{:S(2)}) copy-start(f32[8,128,1024]{2,1,0:T(8,128)} %get-tuple-element.32) | copy-start | bytes 12582916
  111.0 29.5 %all-to-all-start.3 = ((bf16[8,128,512]{2,1,0:T(8,128)(2,1)}), bf16[8,128,512]{2,1,0:T(8,128)(2,1)S(1)}, u32[]{:S(2)}, u32[]{:S(2)}) async-start(bf16[8,128,512]{2,1,0:T(8,128)(2,1)} %bitcast.127), calls=%async_computation.3 | async-start | bytes 2097152 | tf_op jit(solution)/shard_map/all_to_all | solution.py:251
  140.8 5.2 %copy-start.8 = (f32[8,128,1024]{2,1,0:T(8,128)S(1)}, f32[8,128,1024]{2,1,0:T(8,128)}, u32[]{:S(2)}) copy-start(f32[8,128,1024]{2,1,0:T(8,128)} %get-tuple-element.33) | copy-start | bytes 12582916
  142.1 4.0 %copy-start.5 = (f32[8,128,1024]{2,1,0:T(8,128)S(1)}, f32[8,128,1024]{2,1,0:T(8,128)}, u32[]{:S(2)}) copy-start(f32[8,128,1024]{2,1,0:T(8,128)} %get-tuple-element.32) | copy-start | bytes 12582916
  142.1 4.0 %copy-start.17 = (bf16[2,1024,512]{2,1,0:T(8,128)(2,1)S(1)}, bf16[2,1024,512]{2,1,0:T(8,128)(2,1)}, u32[]{:S(2)}) copy-start(bf16[2,1024,512]{2,1,0:T(8,128)(2,1)} %get-tuple-element.53) | copy-start | bytes 6291460
  143.9 51.1 %collective-permute-start.2 = (bf16[128,4096]{1,0:T(8,128)(2,1)}, bf16[128,4096]{1,0:T(8,128)(2,1)S(1)}, u32[]{:S(2)}, u32[]{:S(2)}) collective-permute-start(bf16[128,4096]{1,0:T(8,128)(2,1)} %get-tuple-element.30), channel_id=1, source_target_pairs={{0,24},{8,0},{16,8},{24,16},{1,25},{9,1},{17,9},{25,17},{2,26},{10... | collective-permute-start | bytes 3145736 | tf_op jit(solution)/shard_map/ppermute | solution.py:14
  143.9 51.1 %collective-permute-start.1 = (bf16[128,4096]{1,0:T(8,128)(2,1)}, bf16[128,4096]{1,0:T(8,128)(2,1)}, u32[]{:S(2)}, u32[]{:S(2)}) collective-permute-start(bf16[128,4096]{1,0:T(8,128)(2,1)} %get-tuple-element.31), channel_id=1, source_target_pairs={{0,24},{8,0},{16,8},{24,16},{1,25},{9,1},{17,9},{25,17},{2,26},{10... | collective-permute-start | bytes 3145736 | tf_op jit(solution)/shard_map/ppermute | solution.py:14
  145.5 49.5 %collective-permute-start.3 = (bf16[128,4096]{1,0:T(8,128)(2,1)}, bf16[128,4096]{1,0:T(8,128)(2,1)}, u32[]{:S(2)}, u32[]{:S(2)}) collective-permute-start(bf16[128,4096]{1,0:T(8,128)(2,1)} %get-tuple-element.28), channel_id=1, source_target_pairs={{0,24},{8,0},{16,8},{24,16},{1,25},{9,1},{17,9},{25,17},{2,26},{10... | collective-permute-start | bytes 3145736 | tf_op jit(solution)/shard_map/ppermute | solution.py:14
  145.6 49.4 %collective-permute-start = (bf16[128,4096]{1,0:T(8,128)(2,1)}, bf16[128,4096]{1,0:T(8,128)(2,1)}, u32[]{:S(2)}, u32[]{:S(2)}) collective-permute-start(bf16[128,4096]{1,0:T(8,128)(2,1)} %get-tuple-element.29), channel_id=1, source_target_pairs={{0,8},{8,16},{16,24},{24,0},{1,9},{9,17},{17,25},{25,1},{2,10},{10... | collective-permute-start | bytes 3145736 | tf_op jit(solution)/shard_map/ppermute | solution.py:14
  146.1 4.4 %copy-start.21 = (f32[1024,64]{0,1:T(8,128)S(1)}, f32[1024,64]{0,1:T(8,128)}, u32[]{:S(2)}) copy-start(f32[1024,64]{0,1:T(8,128)} %get-tuple-element.47) | copy-start | bytes 786436
  150.5 3.7 %copy-start.26 = (f32[1024,512]{1,0:T(8,128)}, f32[1024,512]{1,0:T(8,128)S(1)}, u32[]{:S(2)}) copy-start(f32[1024,512]{1,0:T(8,128)S(1)} %get-tuple-element.51) | copy-start | bytes 6291460
  150.5 40.1 %copy-start.10 = (bf16[128,8,512]{2,0,1:T(8,128)(2,1)S(1)}, bf16[128,8,512]{2,0,1:T(8,128)(2,1)}, u32[]{:S(2)}) copy-start(bf16[128,8,512]{2,0,1:T(8,128)(2,1)} %copy-done.9) | copy-start | bytes 3145732
  189.9 1.6 copy-start.27
  (5 other events, 6.2 us)

commit v2 on v0

--- a/solution.py
+++ b/solution.py
@@ -1,8 +1,12 @@
+import functools
 import math
 
 import jax
 import jax.numpy as jnp
+import numpy as np
 from jax import lax
+from jax.experimental import pallas as pl
+from jax.experimental.pallas import tpu as pltpu
 from jax.sharding import PartitionSpec as P
 
 E = 33
@@ -94,7 +98,7 @@
     )
 
 
-def forward_transform(field, tables_all):
+def staged_forward(field, tables_all):
     (
         table_first,
         cos_twist,
@@ -118,7 +122,7 @@
     return contract("sqrp,rkpc->skqc", table_second, twisted)
 
 
-def inverse_transform(spec, tables_all):
+def staged_inverse(spec, tables_all):
     (
         table_first,
         cos_twist,
@@ -145,6 +149,390 @@
     return result.reshape(half_len * inner_len, columns)
 
 
+ROWS = 128
+PAIR = 2 * ROWS
+PADDED = 40
+
+
+def split_tables(length):
+    blocks = length // ROWS
+    fine = np.arange(ROWS)
+    coarse = np.arange(blocks) * ROWS
+    point = np.arange(length)
+    unit = math.pi / (2 * length)
+
+    def pair(count, scale=1.0):
+        angle = unit * (count % (4 * length))
+        return [
+            jnp.asarray((np.cos(angle) * scale).astype(np.float32)),
+            jnp.asarray((np.sin(angle) * scale).astype(np.float32)),
+        ]
+
+    odd = 2 * point + 1
+    ahead = pair((2 * fine + 1)[:, None] * point[None]) + pair((2 * coarse)[:, None] * point[None])
+    back = pair(fine[:, None] * odd[None], 1.0 / length) + pair(coarse[:, None] * odd[None])
+    return ahead + back
+
+
+def padded_features(length):
+    position = np.arange(length)
+    band = np.arange(1, (E - 1) // 2 + 1)
+    angle = 2.0 * math.pi / length * ((band[:, None] ** 2 * position[None]) % length)
+    table = np.zeros((PADDED, length), np.float32)
+    table[0] = position / length
+    table[1 : 1 + len(band)] = np.cos(angle)
+    table[1 + len(band) : E] = np.sin(angle)
+    table[E] = 1.0
+    return table
+
+
+def section_kernel(
+    shards, pipes,
+    v, g1, g2, og, wf, decay, skip, wext, wext_t, feat, feat_t,
+    dc, ds, ec, es, bc, bs, ac, asn,
+    o_next, o_val, o_first, o_second, o_emb, o_wf, o_decay, o_skip,
+    ahead, back, kb, kf, env, kspec, wspec, prod, corr, graw,
+    wsend, usend, wch, uch, mch, gch, mseq, gseq, stage, part, parts,
+    a_send, a_recv, p_send, p_recv, x_send, x_recv,
+):
+    f32, bf16 = jnp.float32, jnp.bfloat16
+    length = shards * ROWS
+    width = wf.shape[1]
+    pipe = lax.axis_index("pipe")
+    me = lax.axis_index("seq")
+    mine = me // 2
+    partner = me + 1 - 2 * (me % 2)
+    pairs = shards // 2
+    nxt = (pipe + 1) % pipes
+    prv = (pipe + pipes - 1) % pipes
+    high = lax.Precision.HIGHEST
+
+    def peer(step, sign):
+        far = 1 + step // 2
+        return ((mine + sign * far + pairs) % pairs) * 2 + step % 2
+
+    def others(sign, visit):
+        def body(step, carry):
+            visit(peer(step, sign))
+            return carry
+
+        lax.fori_loop(0, shards - 2, body, 0)
+        visit(partner)
+
+    def rows(index):
+        return pl.ds(pl.multiple_of(index * ROWS, ROWS), ROWS)
+
+    def cols(index):
+        return pl.ds(pl.multiple_of(index * width, width), width)
+
+    def wide(index):
+        return pl.ds(pl.multiple_of(index * PAIR, PAIR), PAIR)
+
+    def exchange(kind, src, dst, there, source):
+        return pltpu.make_async_remote_copy(
+            src_ref=src, dst_ref=dst, send_sem=a_send.at[kind, there],
+            recv_sem=a_recv.at[kind, source], device_id=(pipe, there),
+            device_id_type=pl.DeviceIdType.MESH,
+        )
+
+    def handed(kind, slot):
+        out = (o_next, o_second, o_val, o_first)[kind]
+        return pltpu.make_async_remote_copy(
+            src_ref=stage.at[kind, slot], dst_ref=out.at[:, cols(slot)],
+            send_sem=p_send.at[kind, slot], recv_sem=p_recv.at[kind, slot],
+            device_id=(nxt if kind == 0 else prv, me),
+            device_id_type=pl.DeviceIdType.MESH,
+        )
+
+    def shared(there, source):
+        return pltpu.make_async_remote_copy(
+            src_ref=part, dst_ref=parts.at[source], send_sem=x_send.at[there],
+            recv_sem=x_recv.at[source], device_id=(pipe, there),
+            device_id_type=pl.DeviceIdType.MESH,
+        )
+
+    def times(one, two, index):
+        return (one[:, cols(index)].astype(f32) * two[:, cols(index)].astype(f32)).astype(bf16)
+
+    barrier = pltpu.get_barrier_semaphore()
+
+    def greet(there):
+        pl.semaphore_signal(
+            barrier, inc=1, device_id=(pipe, there), device_id_type=pl.DeviceIdType.MESH
+        )
+
+    others(1, greet)
+    for side in (nxt, prv):
+        pl.semaphore_signal(
+            barrier, inc=1, device_id=(side, me), device_id_type=pl.DeviceIdType.MESH
+        )
+    pl.semaphore_wait(barrier, shards + 1)
+
+    def send_weighted(there):
+        wsend[there] = times(v, g1, there)
+        exchange(0, wsend.at[there], wch.at[rows(me), :], there, me).start()
+
+    others(1, send_weighted)
+    wch[rows(me), :] = times(v, g1, me)
+
+    def make_kernel(tile, carry):
+        here = wide(tile)
+        step = (lax.broadcasted_iota(jnp.int32, (PAIR, 1), 0) + tile * PAIR).astype(f32)
+        act = jnp.sin(jnp.dot(feat_t[here, :], wext[...], precision=high))
+        envelope = jnp.exp(-decay[...] * step / length) * (1.0 / math.sqrt(length))
+        kernel = jnp.dot(act, wf[...], precision=high) * envelope
+        env[here, :] = envelope
+        kf[here, :] = kernel
+        kb[here, :] = kernel.astype(bf16)
+        return carry
+
+    lax.fori_loop(0, length // PAIR, make_kernel, 0)
+
+    def make_ahead(tile, carry):
+        row_c, row_s = ec[pl.ds(tile, 1), :], es[pl.ds(tile, 1), :]
+        base = pl.multiple_of(tile * PAIR, PAIR)
+        ahead[pl.ds(base, ROWS), :] = (dc[...] * row_c - ds[...] * row_s).astype(bf16)
+        ahead[pl.ds(base + ROWS, ROWS), :] = (-(ds[...] * row_c + dc[...] * row_s)).astype(bf16)
+        return carry
+
+    lax.fori_loop(0, shards, make_ahead, 0)
+
+    def make_kspec(tile, carry):
+        kspec[wide(tile), :] = jnp.dot(
+            ahead[wide(tile), :], kb[...], preferred_element_type=f32
+        )
+        return carry
+
+    lax.fori_loop(0, shards, make_kspec, 0)
+
+    def send_upstream(there):
+        usend[there] = times(og, g2, there)
+        exchange(1, usend.at[there], uch.at[rows(me), :], there, me).start()
+
+    others(1, send_upstream)
+    uch[rows(me), :] = times(og, g2, me)
+
+    def make_back(tile, carry):
+        full_c, full_s = ac[pl.ds(tile, 1), :], asn[pl.ds(tile, 1), :]
+        for block in range(shards):
+            lanes = slice(block * ROWS, (block + 1) * ROWS)
+            row_c, row_s = full_c[:, lanes], full_s[:, lanes]
+            cos_b, sin_b = bc[:, lanes], bs[:, lanes]
+            start = block * PAIR
+            back[rows(tile), start : start + ROWS] = (cos_b * row_c - sin_b * row_s).astype(bf16)
+            back[rows(tile), start + ROWS : start + PAIR] = (
+                -(sin_b * row_c + cos_b * row_s)
+            ).astype(bf16)
+        return carry
+
+    lax.fori_loop(0, shards, make_back, 0)
+
+    others(-1, lambda source: exchange(
+        0, wsend.at[source], wch.at[rows(source), :], source, source).wait_recv())
+
+    def make_product(tile, carry):
+        here = wide(tile)
+        spec = jnp.dot(ahead[here, :], wch[...], preferred_element_type=f32)
+        wspec[here, :] = spec
+        k_re, k_im = kspec[here, :][:ROWS], kspec[here, :][ROWS:]
+        x_re, x_im = spec[:ROWS], spec[ROWS:]
+        prod[here, :] = jnp.concatenate(
+            [k_re * x_re - k_im * x_im, k_re * x_im + k_im * x_re], axis=0
+        ).astype(bf16)
+        return carry
+
+    lax.fori_loop(0, shards, make_product, 0)
+
+    def convolved(kind, field, result, landing):
+        def chunk(index):
+            here = wide(index)
+            conv = jnp.dot(back[here, :], prod[...], preferred_element_type=f32)
+            result[here, :] = (conv + skip[...] * field[here, :].astype(f32)).astype(bf16)
+
+        def far(step, carry):
+            index = (mine + 1 + step) % pairs
+            chunk(index)
+            for side in range(2):
+                there = index * 2 + side
+                exchange(kind, result.at[rows(there), :], landing.at[me], there, me).start()
+            return carry
+
+        lax.fori_loop(0, pairs - 1, far, 0)
+        chunk(mine)
+        exchange(kind, result.at[rows(partner), :], landing.at[me], partner, me).start()
+        landing[me] = result[rows(me), :]
+
+    convolved(2, wch, mch, mseq)
+
+    others(-1, lambda source: exchange(
+        1, usend.at[source], uch.at[rows(source), :], source, source).wait_recv())
+
+    def make_products(tile, carry):
+        here = wide(tile)
+        spec = jnp.dot(ahead[here, :], uch[...], preferred_element_type=f32)
+        x_re, x_im = spec[:ROWS], spec[ROWS:]
+        for left, target in ((kspec, prod), (wspec, corr)):
+            l_re, l_im = left[here, :][:ROWS], left[here, :][ROWS:]
+            target[here, :] = jnp.concatenate(
+                [l_re * x_re + l_im * x_im, l_re * x_im - l_im * x_re], axis=0
+            ).astype(bf16)
+        return carry
+
+    lax.fori_loop(0, shards, make_products, 0)
+    convolved(3, uch, gch, gseq)
+
+    def pass_mixed(source):
+        block = mseq[source].astype(f32)
+        stage[0, source] = (g2[:, cols(source)].astype(f32) * block).astype(bf16)
+        stage[1, source] = (og[:, cols(source)].astype(f32) * block).astype(bf16)
+        handed(0, source).start()
+        handed(1, source).start()
+
+    def land_mixed(source):
+        exchange(2, mch.at[rows(source), :], mseq.at[source], source, source).wait_recv()
+        pass_mixed(source)
+
+    pass_mixed(me)
+    others(-1, land_mixed)
+
+    def correlate(tile, carry):
+        here = wide(tile)
+        step = (lax.broadcasted_iota(jnp.int32, (PAIR, 1), 0) + tile * PAIR).astype(f32)
+        grad = jnp.dot(back[here, :], corr[...], preferred_element_type=f32)
+        graw[here, :] = (grad * env[here, :]).astype(bf16)
+        sum_d, sum_s = carry
+        sum_d += jnp.sum(grad * kf[here, :] * (-step / length), axis=0, keepdims=True)
+        both = uch[here, :].astype(f32) * wch[here, :].astype(f32)
+        return sum_d, sum_s + jnp.sum(both, axis=0, keepdims=True)
+
+    empty = jnp.zeros((1, width), f32)
+    sum_d, sum_s = lax.fori_loop(0, length // PAIR, correlate, (empty, empty))
+    o_decay[...] = sum_d
+    o_skip[...] = sum_s
+
+    def halves(value):
+        top = value.astype(bf16)
+        return jnp.concatenate([top, (value - top.astype(f32)).astype(bf16)], axis=0)
+
+    hidden = wext_t.shape[0]
+    preact = jnp.dot(wext_t[...], feat[...], precision=high)
+    both = jnp.dot(halves(jnp.sin(preact)), graw[...], preferred_element_type=f32)
+    o_wf[...] = both[:hidden] + both[hidden:]
+    both = lax.dot_general(
+        halves(wf[...]), graw[...], (((1,), (1,)), ((), ())), preferred_element_type=f32
+    )
+    grad_pre = (both[:hidden] + both[hidden:]) * jnp.cos(preact)
+    part[...] = lax.dot_general(
+        feat[...], jnp.concatenate([grad_pre, jnp.zeros_like(grad_pre)], axis=0),
+        (((1,), (1,)), ((), ())), precision=high,
+    )
+    others(1, lambda there: shared(there, me).start())
+
+    def pass_grad(source):
+        block = gseq[source].astype(f32)
+        stage[2, source] = (g1[:, cols(source)].astype(f32) * block).astype(bf16)
+        stage[3, source] = (v[:, cols(source)].astype(f32) * block).astype(bf16)
+        handed(2, source).start()
+        handed(3, source).start()
+
+    def land_grad(source):
+        exchange(3, gch.at[rows(source), :], gseq.at[source], source, source).wait_recv()
+        pass_grad(source)
+
+    pass_grad(me)
+    others(-1, land_grad)
+
+    parts[me] = part[...]
+    others(-1, lambda source: shared(source, source).wait_recv())
+    total = parts[0]
+    for index in range(1, shards):
+        total = total + parts[index]
+    o_emb[...] = total
+
+    def sent(there):
+        exchange(0, wsend.at[there], wch.at[rows(me), :], there, me).wait_send()
+        exchange(1, usend.at[there], uch.at[rows(me), :], there, me).wait_send()
+        exchange(2, mch.at[rows(there), :], mseq.at[me], there, me).wait_send()
+        exchange(3, gch.at[rows(there), :], gseq.at[me], there, me).wait_send()
+        shared(there, me).wait_send()
+
+    others(1, sent)
+
+    def finish(slot, carry):
+        for kind in range(4):
+            handed(kind, slot).wait()
+        return carry
+
+    lax.fori_loop(0, shards, finish, 0)
+
+
+def fused_section(v, g1, g2, og, w_embed, b_embed, wf, decay, skip):
+    shards = lax.axis_size("seq")
+    pipes = lax.axis_size("pipe")
+    length = shards * ROWS
+    wide_cols = v.shape[1]
+    width = wf.shape[1]
+    hidden = wf.shape[0]
+    f32, bf16 = jnp.float32, jnp.bfloat16
+    wext = jnp.concatenate(
+        [w_embed, b_embed[None], jnp.zeros((PADDED - E - 1, hidden), f32)], axis=0
+    )
+    feat = padded_features(length)
+    tables = split_tables(length)
+    vmem = pl.BlockSpec(memory_space=pltpu.VMEM)
+    hbm = pl.BlockSpec(memory_space=pl.ANY)
+    stream = jax.ShapeDtypeStruct((ROWS, wide_cols), bf16)
+    row = jax.ShapeDtypeStruct((1, width), f32)
+    dma = pltpu.SemaphoreType.DMA
+    results = pl.pallas_call(
+        functools.partial(section_kernel, shards, pipes),
+        out_shape=(
+            stream, stream, stream, stream,
+            jax.ShapeDtypeStruct((PADDED, 2 * hidden), f32),
+            jax.ShapeDtypeStruct((hidden, width), f32), row, row,
+        ),
+        in_specs=[vmem] * 19,
+        out_specs=(hbm,) * 4 + (vmem,) * 4,
+        scratch_shapes=[
+            pltpu.VMEM((2 * length, length), bf16),
+            pltpu.VMEM((length, 2 * length), bf16),
+            pltpu.VMEM((length, width), bf16),
+            pltpu.VMEM((length, width), f32),
+            pltpu.VMEM((length, width), f32),
+            pltpu.VMEM((2 * length, width), f32),
+            pltpu.VMEM((2 * length, width), f32),
+            pltpu.VMEM((2 * length, width), bf16),
+            pltpu.VMEM((2 * length, width), bf16),
+            pltpu.VMEM((length, width), bf16),
+            pltpu.VMEM((shards, ROWS, width), bf16),
+            pltpu.VMEM((shards, ROWS, width), bf16),
+            pltpu.VMEM((length, width), bf16),
+            pltpu.VMEM((length, width), bf16),
+            pltpu.VMEM((length, width), bf16),
+            pltpu.VMEM((length, width), bf16),
+            pltpu.VMEM((shards, ROWS, width), bf16),
+            pltpu.VMEM((shards, ROWS, width), bf16),
+            pltpu.VMEM((4, shards, ROWS, width), bf16),
+            pltpu.VMEM((PADDED, 2 * hidden), f32),
+            pltpu.VMEM((shards, PADDED, 2 * hidden), f32),
+            dma((4, shards)), dma((4, shards)),
+            dma((4, shards)), dma((4, shards)),
+            dma((shards,)), dma((shards,)),
+        ],
+        compiler_params=pltpu.CompilerParams(
+            collective_id=0, has_side_effects=True, vmem_limit_bytes=60 * 1024 * 1024
+        ),
+    )(
+        v, g1, g2, og, wf, decay[None], skip[None], wext, wext.T,
+        jnp.asarray(feat), jnp.asarray(feat.T.copy()), *tables,
+    )
+    moved_next, moved_val, moved_first, moved_second, emb, grad_wf, grad_d, grad_s = results
+    return (
+        moved_next[None], moved_val[None], moved_first[None], moved_second[None],
+        emb[None, :E, :hidden], emb[None, E, :hidden], grad_wf[None], grad_d, grad_s,
+    )
+
+
 def spectral_product(left, right, conjugate_left):
     left_re = left[0]
     left_im = left[1]
@@ -165,6 +553,11 @@
     filter_w = w_filter[0]
     shards = lax.axis_size("seq")
     length = values.shape[0] * shards
+    if length <= 1024 and values.shape[0] == ROWS and shards % 2 == 0 and lax.axis_size("pipe") > 2:
+        return fused_section(
+            values, gate_first, gate_second, cotangent,
+            w_embed[0], b_embed[0], filter_w, decay[0], skip[0],
+        )
     weighted = (values.astype(jnp.float32) * gate_first.astype(jnp.float32)).astype(jnp.bfloat16)
     upstream = (cotangent.astype(jnp.float32) * gate_second.astype(jnp.float32)).astype(
         jnp.bfloat16
@@ -176,6 +569,7 @@
     envelope = jnp.exp(-decay[0][None, :] * positions / length) * (1.0 / math.sqrt(length))
     kernel = contract("ft,fc->tc", activation, filter_w) * envelope
     tables_all = build_tables(length)
+    forward_transform, inverse_transform = staged_forward, staged_inverse
     kernel_spec = forward_transform(kernel, tables_all)
     skip_row = skip[0][None, :]
     weighted_chan, upstream_chan = (

time: 287 us -> 143 us (0.50)
  the two profiles are of different devices: /device:TPU:0 before, /device:TPU:29 now
where the time goes in v2:
time: 143 us
  Pallas kernels  128 us (90%)
  local copies, waits for them, and re-layouts  13.4 us (9%)
    pallas_call x1, Pallas kernels, fused_section(): pl.pallas_call(functools.partial(section_kernel, shards, pipes), out_shap...  128 us
    unnamed x24, local copies, waits for them, and re-layouts  10.7 us

profile of v2, /device:TPU:29, one launch (start us, length us, event | category | flops | bytes accessed | tf_op | source)
XLA Modules:
  0.0 142.7 jit_solution(17455985109863864571)
XLA Ops:
  0.6 0.8 copy.28
  1.4 0.0 copy-start.6
  1.4 0.7 copy-done.6
  2.1 0.1 copy.29
  2.2 0.1 pad.2.clone
  2.3 0.1 maximum_maximum_fusion
  2.4 0.7 copy.30.wext
  3.0 0.7 fusion.wext_t
  3.7 127.8 %shard_map.250 = (bf16[128,4096]{1,0:T(8,128)(2,1)}, bf16[128,4096]{1,0:T(8,128)(2,1)}, bf16[128,4096]{1,0:T(8,128)(2,1)}, bf16[128,4096]{1,0:T(8,128)(2,1)}, f3...) custom-call(bf16[128,4096]{1,0:T(8,128)(2,1)} %bitcast.19, ...), custom_call_target="tpu_custom_call" | custom-call | tf_op jit(solution)/shard_map/pallas_call | solution.py:487
  131.6 0.7 slice_bitcast_fusion
  132.3 0.6 copy.31
  132.9 1.2 slice.7
  134.1 0.0 copy-start.2
  134.1 2.4 %copy.39 = bf16[1,128,4096]{2,1,0:T(8,128)(2,1)} copy(bf16[1,128,4096]{2,1,0:T(8,128)(2,1)} %bitcast.18) | data formatting | bytes 2097152
  136.5 0.0 copy-done.2
  136.5 0.0 copy-start.1
  136.5 1.0 copy.40
  137.5 0.6 copy-done.1
  138.1 0.0 copy-start
  138.1 1.0 copy.41
  139.1 0.6 copy-done
  139.7 0.0 copy-start.3
  139.7 1.0 copy.42
  140.7 0.1 copy-done.3
  140.7 0.0 copy-start.5
  140.7 0.7 copy.43
  141.4 0.0 copy-done.5
  141.4 0.0 copy-start.4
  141.4 0.6 copy.44
  142.0 0.1 copy-done.4
  142.1 0.6 copy.45
  (1 shorter events, 0.0 us)
Async XLA Ops:
  1.4 0.7 copy-start.6
  134.1 2.4 %copy-start.2 = (bf16[128,4096]{1,0:T(8,128)(2,1)S(1)}, bf16[128,4096]{1,0:T(8,128)(2,1)}, u32[]{:S(2)}) copy-start(bf16[128,4096]{1,0:T(8,128)(2,1)} %get-tuple-element.18) | copy-start | bytes 3145732
  136.5 1.6 %copy-start.1 = (bf16[128,4096]{1,0:T(8,128)(2,1)S(1)}, bf16[128,4096]{1,0:T(8,128)(2,1)}, u32[]{:S(2)}) copy-start(bf16[128,4096]{1,0:T(8,128)(2,1)} %get-tuple-element.19) | copy-start | bytes 3145732
  138.1 1.6 %copy-start = (bf16[128,4096]{1,0:T(8,128)(2,1)S(1)}, bf16[128,4096]{1,0:T(8,128)(2,1)}, u32[]{:S(2)}) copy-start(bf16[128,4096]{1,0:T(8,128)(2,1)} %get-tuple-element.20) | copy-start | bytes 3145732
  139.7 1.0 copy-start.3
  140.7 0.7 copy-start.5
  141.4 0.7 copy-start.4

commit v3 on v2

--- a/solution.py
+++ b/solution.py
@@ -188,11 +188,13 @@
 
 def section_kernel(
     shards, pipes,
-    v, g1, g2, og, wf, decay, skip, wext, wext_t, feat, feat_t,
-    dc, ds, ec, es, bc, bs, ac, asn,
+    v_in, g1_in, g2_in, og_in, feat_in, feat_t_in,
+    dc_in, ds_in, ec_in, es_in, bc_in, bs_in, ac_in, asn_in,
+    wf, decay, skip, w_t, bias,
     o_next, o_val, o_first, o_second, o_emb, o_wf, o_decay, o_skip,
     ahead, back, kb, kf, env, kspec, wspec, prod, corr, graw,
     wsend, usend, wch, uch, mch, gch, mseq, gseq, stage, part, parts,
+    v, g1, og, g2, feat_t, dc, ds, ec, es, bc, bs, ac, asn, feat, wext_t, loaded,
     a_send, a_recv, p_send, p_recv, x_send, x_recv,
 ):
     f32, bf16 = jnp.float32, jnp.bfloat16
@@ -254,6 +256,16 @@
     def times(one, two, index):
         return (one[:, cols(index)].astype(f32) * two[:, cols(index)].astype(f32)).astype(bf16)
 
+    loads = [
+        pltpu.make_async_copy(src, dst, loaded.at[index])
+        for index, (src, dst) in enumerate((
+            (v_in, v), (g1_in, g1), (feat_t_in, feat_t), (dc_in, dc), (ds_in, ds), (ec_in, ec),
+            (es_in, es), (og_in, og), (g2_in, g2), (bc_in, bc), (bs_in, bs), (ac_in, ac),
+            (asn_in, asn), (feat_in, feat),
+        ))
+    ]
+    for load in loads:
+        load.start()
     barrier = pltpu.get_barrier_semaphore()
 
     def greet(there):
@@ -266,6 +278,15 @@
         pl.semaphore_signal(
             barrier, inc=1, device_id=(side, me), device_id_type=pl.DeviceIdType.MESH
         )
+    hidden = wf.shape[0]
+    lane = lax.broadcasted_iota(jnp.int32, (hidden, hidden), 1)
+    line = lax.broadcasted_iota(jnp.int32, (hidden, hidden), 0)
+    column = jnp.sum(jnp.where(lane == line, bias[...], 0.0), axis=1, keepdims=True)
+    wext_t[...] = jnp.zeros_like(wext_t)
+    wext_t[:, :E] = w_t[...]
+    wext_t[:, E : E + 1] = column
+    for load in loads[:2]:
+        load.wait()
     pl.semaphore_wait(barrier, shards + 1)
 
     def send_weighted(there):
@@ -275,10 +296,15 @@
     others(1, send_weighted)
     wch[rows(me), :] = times(v, g1, me)
 
+    for load in loads[2:7]:
+        load.wait()
+
     def make_kernel(tile, carry):
         here = wide(tile)
         step = (lax.broadcasted_iota(jnp.int32, (PAIR, 1), 0) + tile * PAIR).astype(f32)
-        act = jnp.sin(jnp.dot(feat_t[here, :], wext[...], precision=high))
+        act = jnp.sin(lax.dot_general(
+            feat_t[here, :], wext_t[...], (((1,), (1,)), ((), ())), precision=high
+        ))
         envelope = jnp.exp(-decay[...] * step / length) * (1.0 / math.sqrt(length))
         kernel = jnp.dot(act, wf[...], precision=high) * envelope
         env[here, :] = envelope
@@ -304,6 +330,9 @@
         return carry
 
     lax.fori_loop(0, shards, make_kspec, 0)
+
+    for load in loads[7:]:
+        load.wait()
 
     def send_upstream(there):
         usend[there] = times(og, g2, there)
@@ -414,7 +443,6 @@
         top = value.astype(bf16)
         return jnp.concatenate([top, (value - top.astype(f32)).astype(bf16)], axis=0)
 
-    hidden = wext_t.shape[0]
     preact = jnp.dot(wext_t[...], feat[...], precision=high)
     both = jnp.dot(halves(jnp.sin(preact)), graw[...], preferred_element_type=f32)
     o_wf[...] = both[:hidden] + both[hidden:]
@@ -464,6 +492,38 @@
         return carry
 
     lax.fori_loop(0, shards, finish, 0)
+
+
+CHUNKS = 4
+
+
+def finish_kernel(
+    a_in, b_in, c_in, d_in, emb, wf, row_d, row_s,
+    a_out, b_out, c_out, d_out, o_emb, o_bias, o_wf, o_d, o_s, held, got, put,
+):
+    rows = ROWS // CHUNKS
+    reads, writes = [], []
+    for kind, (src, dst) in enumerate(
+        ((a_in, a_out), (b_in, b_out), (c_in, c_out), (d_in, d_out))
+    ):
+        for chunk in range(CHUNKS):
+            here = pl.ds(chunk * rows, rows)
+            index = kind * CHUNKS + chunk
+            middle = held.at[kind, here, :]
+            reads.append(pltpu.make_async_copy(src.at[here, :], middle, got.at[index]))
+            writes.append(pltpu.make_async_copy(middle, dst.at[0, here, :], put.at[index]))
+    for read in reads:
+        read.start()
+    o_emb[0] = emb[:E, : o_emb.shape[2]]
+    o_bias[...] = emb[E : E + 1, : o_bias.shape[1]]
+    o_wf[0] = wf[...]
+    o_d[...] = row_d[...]
+    o_s[...] = row_s[...]
+    for read, write in zip(reads, writes):
+        read.wait()
+        write.start()
+    for write in writes:
+        write.wait()
 
 
 def fused_section(v, g1, g2, og, w_embed, b_embed, wf, decay, skip):
@@ -474,9 +534,6 @@
     width = wf.shape[1]
     hidden = wf.shape[0]
     f32, bf16 = jnp.float32, jnp.bfloat16
-    wext = jnp.concatenate(
-        [w_embed, b_embed[None], jnp.zeros((PADDED - E - 1, hidden), f32)], axis=0
-    )
     feat = padded_features(length)
     tables = split_tables(length)
     vmem = pl.BlockSpec(memory_space=pltpu.VMEM)
@@ -491,7 +548,7 @@
             jax.ShapeDtypeStruct((PADDED, 2 * hidden), f32),
             jax.ShapeDtypeStruct((hidden, width), f32), row, row,
         ),
-        in_specs=[vmem] * 19,
+        in_specs=[hbm] * 14 + [vmem] * 5,
         out_specs=(hbm,) * 4 + (vmem,) * 4,
         scratch_shapes=[
             pltpu.VMEM((2 * length, length), bf16),
@@ -515,6 +572,15 @@
             pltpu.VMEM((4, shards, ROWS, width), bf16),
             pltpu.VMEM((PADDED, 2 * hidden), f32),
             pltpu.VMEM((shards, PADDED, 2 * hidden), f32),
+            *[pltpu.VMEM((ROWS, wide_cols), bf16)] * 4,
+            pltpu.VMEM((length, PADDED), f32),
+            *[pltpu.VMEM((ROWS, length), f32)] * 2,
+            *[pltpu.VMEM((shards, length), f32)] * 2,
+            *[pltpu.VMEM((ROWS, length), f32)] * 2,
+            *[pltpu.VMEM((shards, length), f32)] * 2,
+            pltpu.VMEM((PADDED, length), f32),
+            pltpu.VMEM((hidden, PADDED), f32),
+            dma((14,)),
             dma((4, shards)), dma((4, shards)),
             dma((4, shards)), dma((4, shards)),
             dma((shards,)), dma((shards,)),
@@ -523,13 +589,27 @@
             collective_id=0, has_side_effects=True, vmem_limit_bytes=60 * 1024 * 1024
         ),
     )(
-        v, g1, g2, og, wf, decay[None], skip[None], wext, wext.T,
-        jnp.asarray(feat), jnp.asarray(feat.T.copy()), *tables,
-    )
-    moved_next, moved_val, moved_first, moved_second, emb, grad_wf, grad_d, grad_s = results
-    return (
-        moved_next[None], moved_val[None], moved_first[None], moved_second[None],
-        emb[None, :E, :hidden], emb[None, E, :hidden], grad_wf[None], grad_d, grad_s,
+        v, g1, g2, og, jnp.asarray(feat), jnp.asarray(feat.T.copy()), *tables,
+        wf, decay[None], skip[None], w_embed.T, b_embed[None],
+    )
+    final = jax.ShapeDtypeStruct((1, ROWS, wide_cols), bf16)
+    return tuple(
+        pl.pallas_call(
+            finish_kernel,
+            out_shape=(
+                final, final, final, final,
+                jax.ShapeDtypeStruct((1, E, hidden), f32),
+                jax.ShapeDtypeStruct((1, hidden), f32),
+                jax.ShapeDtypeStruct((1, hidden, width), f32), row, row,
+            ),
+            in_specs=[hbm] * 4 + [vmem] * 4,
+            out_specs=(hbm,) * 4 + (vmem,) * 5,
+            scratch_shapes=[
+                pltpu.VMEM((4, ROWS, wide_cols), bf16),
+                dma((4 * CHUNKS,)), dma((4 * CHUNKS,)),
+            ],
+            compiler_params=pltpu.CompilerParams(vmem_limit_bytes=60 * 1024 * 1024),
+        )(*results)
     )
 
 

time: 143 us -> 135 us (0.944)
  local copies, waits for them, and re-layouts: 13.4 us -> 2.77 us
  Pallas kernels: 128 us -> 131 us
    unnamed x24 -> x1, local copies, waits for them, and re-layouts: 10.7 us -> 1.42 us
    pallas_call x0 -> x1, Pallas kernels: none -> 5.44 us  [fused_section(): pl.pallas_call(finish_kernel, out_shape=(final, final, final, final, jax....]
    pallas_call x1, Pallas kernels: 128 us -> 126 us  [fused_section(): pl.pallas_call(functools.partial(section_kernel, shards, pipes), out_shap...]
where the time goes in v3:
time: 135 us
  Pallas kernels  131 us (97%)
  local copies, waits for them, and re-layouts  2.77 us (2%)
    pallas_call x1, Pallas kernels, fused_section(): pl.pallas_call(functools.partial(section_kernel, shards, pipes), out_shap...  126 us
    pallas_call x1, Pallas kernels, fused_section(): pl.pallas_call(finish_kernel, out_shape=(final, final, final, final, jax....  5.44 us

profile of v3, /device:TPU:29, one launch (start us, length us, event | category | flops | bytes accessed | tf_op | source)
XLA Modules:
  0.0 134.8 jit_solution(6421122514057810371)
XLA Ops:
  0.6 1.4 %copy.28 = f32[1,33,64]{1,2,0:T(8,128)} copy(f32[1,33,64]{2,0,1:T(1,128)} %param.23) | data formatting | bytes 16896 | tf_op args[4]
  2.1 125.9 %shard_map.250 = (bf16[128,4096]{1,0:T(8,128)(2,1)}, bf16[128,4096]{1,0:T(8,128)(2,1)}, bf16[128,4096]{1,0:T(8,128)(2,1)}, bf16[128,4096]{1,0:T(8,128)(2,1)}, f3...) custom-call(bf16[128,4096]{1,0:T(8,128)(2,1)} %bitcast.8, ...), custom_call_target="tpu_custom_call" | custom-call | tf_op jit(solution)/shard_map/pallas_call | solution.py:544
  128.0 5.4 %shard_map.251 = (bf16[1,128,4096]{2,1,0:T(8,128)(2,1)}, bf16[1,128,4096]{2,1,0:T(8,128)(2,1)}, bf16[1,128,4096]{2,1,0:T(8,128)(2,1)}, bf16[1,128,4096]{2,1,0:T(...) custom-call(bf16[128,4096]{1,0:T(8,128)(2,1)} %get-tuple-element.17., ...), custom_call_target="tpu_custom_call" | custom-call | tf_op jit(solution)/shard_map/pallas_call | solution.py:597
  133.4 1.4 %copy.29 = f32[1,33,64]{2,0,1:T(1,128)} copy(f32[1,33,64]{2,1,0:T(8,128)} %get-tuple-element.29) | data formatting | bytes 16896 | tf_op jit(solution)/shard_map/pallas_call | solution.py:597

commit v4 on v3

--- a/solution.py
+++ b/solution.py
@@ -334,13 +334,6 @@
     for load in loads[7:]:
         load.wait()
 
-    def send_upstream(there):
-        usend[there] = times(og, g2, there)
-        exchange(1, usend.at[there], uch.at[rows(me), :], there, me).start()
-
-    others(1, send_upstream)
-    uch[rows(me), :] = times(og, g2, me)
-
     def make_back(tile, carry):
         full_c, full_s = ac[pl.ds(tile, 1), :], asn[pl.ds(tile, 1), :]
         for block in range(shards):
@@ -356,6 +349,14 @@
 
     lax.fori_loop(0, shards, make_back, 0)
 
+    def send_upstream(there):
+        usend[there] = times(og, g2, there)
+        exchange(0, wsend.at[there], wch.at[rows(me), :], there, me).wait_send()
+        exchange(1, usend.at[there], uch.at[rows(me), :], there, me).start()
+
+    others(1, send_upstream)
+    uch[rows(me), :] = times(og, g2, me)
+
     others(-1, lambda source: exchange(
         0, wsend.at[source], wch.at[rows(source), :], source, source).wait_recv())
 
@@ -478,7 +479,6 @@
     o_emb[...] = total
 
     def sent(there):
-        exchange(0, wsend.at[there], wch.at[rows(me), :], there, me).wait_send()
         exchange(1, usend.at[there], uch.at[rows(me), :], there, me).wait_send()
         exchange(2, mch.at[rows(there), :], mseq.at[me], there, me).wait_send()
         exchange(3, gch.at[rows(there), :], gseq.at[me], there, me).wait_send()

time: 135 us -> 135 us (level)
  no operation moved by 1% of the time
where the time goes in v4:
time: 135 us
  Pallas kernels  131 us (97%)
  local copies, waits for them, and re-layouts  2.77 us (2%)
    pallas_call x1, Pallas kernels, fused_section(): pl.pallas_call(functools.partial(section_kernel, shards, pipes), out_shap...  126 us
    pallas_call x1, Pallas kernels, fused_section(): pl.pallas_call(finish_kernel, out_shape=(final, final, final, final, jax....  5.44 us

profile of v4, /device:TPU:29, one launch (start us, length us, event | category | flops | bytes accessed | tf_op | source)
XLA Modules:
  0.0 134.7 jit_solution(10330527084592264915)
XLA Ops:
  0.6 1.4 %copy.28 = f32[1,33,64]{1,2,0:T(8,128)} copy(f32[1,33,64]{2,0,1:T(1,128)} %param.23) | data formatting | bytes 16896 | tf_op args[4]
  2.1 125.8 %shard_map.250 = (bf16[128,4096]{1,0:T(8,128)(2,1)}, bf16[128,4096]{1,0:T(8,128)(2,1)}, bf16[128,4096]{1,0:T(8,128)(2,1)}, bf16[128,4096]{1,0:T(8,128)(2,1)}, f3...) custom-call(bf16[128,4096]{1,0:T(8,128)(2,1)} %bitcast.8, ...), custom_call_target="tpu_custom_call" | custom-call | tf_op jit(solution)/shard_map/pallas_call | solution.py:544
  127.9 5.4 %shard_map.251 = (bf16[1,128,4096]{2,1,0:T(8,128)(2,1)}, bf16[1,128,4096]{2,1,0:T(8,128)(2,1)}, bf16[1,128,4096]{2,1,0:T(8,128)(2,1)}, bf16[1,128,4096]{2,1,0:T(...) custom-call(bf16[128,4096]{1,0:T(8,128)(2,1)} %get-tuple-element.17., ...), custom_call_target="tpu_custom_call" | custom-call | tf_op jit(solution)/shard_map/pallas_call | solution.py:597
  133.4 1.4 %copy.29 = f32[1,33,64]{2,0,1:T(1,128)} copy(f32[1,33,64]{2,1,0:T(8,128)} %get-tuple-element.29) | data formatting | bytes 16896 | tf_op jit(solution)/shard_map/pallas_call | solution.py:597
